TPU v7x, 256 devices: a whole 4x4x8 slice. The times are simulated.
256 devices in a mesh: tm: 128 (over x_hi, z, y, core), mp: 2 (over x_lo).
Axes of the slice: x: 4 (x_hi: 2, x_lo: 2; x = x_hi * 2 + x_lo), y: 4, z: 8, core: 2. Of those that a mesh axis runs over, the one named last changes fastest.
Arguments:
- latent_picture_tokens: bfloat16 [256, 384, 768], P(('tm', 'mp')), may hold values from -6 to 6
- mixing_rescale_factor: float32 [2, 768], replicated, may hold values from 0.1 to 1.9
- joint_lookup_matrix: bfloat16 [2, 768, 1280], P(None, None, 'mp')
- score_scaling: float32 [2, 6], replicated, may hold values from 1 to 24
- mixing_return_matrix: bfloat16 [2, 768, 768], P(None, 'mp'), may hold values from -0.21875 to 0.21875
- perceptron_rescale_factor: float32 [2, 768], replicated, may hold values from 0.1 to 1.9
- widening_matrix: bfloat16 [2, 768, 1536], P(None, None, 'mp'), may hold values from -0.21875 to 0.21875
- narrowing_matrix: bfloat16 [2, 1536, 768], P(None, 'mp'), may hold values from -0.15625 to 0.15625
Outputs:
- result: bfloat16 [256, 384, 768], P(('tm', 'mp'))
All inputs are finite; a program needn't handle non-finite values.
Results may differ from a plain program's by a relative error of at most 0.033.
Values may be sent and summed in bfloat16 or wider, within the bound.
No kernel may reach another device: no remote copies, remote signals or barrier semaphores. Data moves between devices by JAX's collectives and lax.ppermute only.
A program may use at most 128 MiB of HBM per device.

v0:
```python
import functools
import math

import jax
import jax.numpy as jnp
from jax import lax
from jax.experimental import pallas as pl
from jax.experimental.pallas import tpu as pltpu
from jax.sharding import PartitionSpec as P


HEAD = 128
RATIO = 3
S = 384
D = 768
G = (RATIO + 2) * HEAD
BOTH = ("tm", "mp")
COUNT = 256
BF = jnp.bfloat16
F32 = jnp.float32
QSCALE = 1.0 / (math.sqrt(HEAD) * math.log(2.0))


def place(i):
    return (i >> 7) * 2 + (i & 1), (i >> 2) & 3, (i >> 4) & 7, (i >> 1) & 1


def index(x, y, z, c):
    return ((x >> 1) << 7) | (z << 4) | (y << 2) | (c << 1) | (x & 1)


def pairs(fn):
    return [(i, index(*fn(*place(i)))) for i in range(COUNT)]


X1 = pairs(lambda x, y, z, c: (x ^ 1, y, z, c))
X3 = pairs(lambda x, y, z, c: (x ^ 3, y, z, c))
Y1 = pairs(lambda x, y, z, c: (x, y ^ 1, z, c))
Y3 = pairs(lambda x, y, z, c: (x, y ^ 3, z, c))
Z1 = pairs(lambda x, y, z, c: (x, y, z ^ 1, c))
Z2 = pairs(lambda x, y, z, c: (x, y, z ^ 2, c))
Z6 = pairs(lambda x, y, z, c: (x, y, (((z + 2) & 7) ^ 2) - 2 & 7, c))
CORE = pairs(lambda x, y, z, c: (x, y, z, 1 - c))
NEXT = [(i, i + 1) for i in range(COUNT - 1)]


def send(v, p):
    return lax.ppermute(v, BOTH, p)


def spread_first(x, p, joint):
    me = lax.axis_index(BOTH)
    px, py, pz, pc = (me >> 7) * 2 + (me & 1), (me >> 2) & 3, (me >> 4) & 7, (me >> 1) & 1
    tie = lax.optimization_barrier
    half = D // 2
    got = send(x[:, half:], CORE)
    cur = jnp.where(pc == 0, x[:, :half], got)
    cur, p = tie((cur, p))
    q0 = fetch(p[0], None)
    cur = jnp.where(py == 0, cur[:192], send(cur[192:], Y3))
    cur = jnp.where((py == 0) | (py == 3), cur[:96], send(cur[96:], Y1))
    cur, q0 = tie((cur, q0))
    q0 = swap(q0)
    cur = jnp.where(pz == 0, cur[:48], send(cur[48:], Z1))
    cur = jnp.where(px == 0, cur, send(cur, X1))
    cur, q0 = tie((cur, q0))
    q, kv = joint(0, x, q0)
    cur = jnp.where(px < 2, cur, send(cur, X3))
    cur, kv = tie((cur, kv))
    prior = send(kv, NEXT)
    r0 = fetch(p[1], cur)
    a, b = send(cur, Z2), send(cur, Z6)
    cur = jnp.where(pz < 2, cur, jnp.where(pz < 4, a, b))
    got = send(cur, Z6)
    cur = jnp.where((pz == 4) | (pz == 5), got, cur)
    cur = jnp.concatenate([cur, send(cur, Z1)], axis=0)
    q1 = fetch(p[2], kv)
    cur = jnp.concatenate([cur, send(cur, Y1)], axis=0)
    cur = jnp.concatenate([cur, send(cur, Y3)], axis=0)
    got = send(cur, CORE)
    whole = jnp.where(
        pc == 0, jnp.concatenate([cur, got], axis=1), jnp.concatenate([got, cur], axis=1)
    )
    return whole, q, kv, prior, q0, r0, q1


VMEM = pl.BlockSpec(memory_space=pltpu.VMEM)
SMEM = pl.BlockSpec(memory_space=pltpu.SMEM)
ANY = pl.BlockSpec(memory_space=pl.ANY)
HBM = pl.BlockSpec(memory_space=pltpu.HBM)
NQ, NO, NU = 192, 96, 192


def params(mib=40):
    return pltpu.CompilerParams(vmem_limit_bytes=mib << 20)


def cost(flops, nbytes):
    return pl.CostEstimate(flops=flops, bytes_accessed=nbytes, transcendentals=0)


def cut_kernel(parts, info, *refs):
    k = 1 + max(i for part in parts for i, _, _ in part)
    n = len(parts)
    sources, outs, stages, sems = refs[:k], refs[k : k + 2 * n], refs[k + 2 * n : -1], refs[-1]
    core = info[0]
    at = 0
    loads = []
    for stage, part in zip(stages, parts):
        for j in range(2):
            to = 0
            group = []
            for i, l, rows in part:
                row = pl.multiple_of(core * (2 * rows) + j * rows, 16)
                group.append(
                    bring(
                        sources[i].at[l, pl.ds(row, rows)],
                        stage.at[j, pl.ds(to, rows)],
                        sems.at[at],
                    )
                )
                to += rows
                at += 1
            loads.append(group)
    stores = []
    for m, group in enumerate(loads):
        wait(group)
        stores.append(bring(stages[m // 2].at[m % 2], outs[m], sems.at[at]))
        at += 1
    wait(stores)


def cut(info, sources, parts):
    widths = [sources[part[0][0]].shape[2] for part in parts]
    heights = [sum(rows for _, _, rows in part) for part in parts]
    shapes = []
    for n, w in zip(heights, widths):
        shapes += [jax.ShapeDtypeStruct((n, w), BF)] * 2
    flat = pl.pallas_call(
        functools.partial(cut_kernel, parts),
        out_shape=shapes,
        in_specs=[SMEM] + [HBM] * len(sources),
        out_specs=[HBM] * len(shapes),
        scratch_shapes=[pltpu.VMEM((2, n, w), BF) for n, w in zip(heights, widths)]
        + [pltpu.SemaphoreType.DMA((2 * sum(len(part) + 1 for part in parts),))],
        compiler_params=params(63),
        name="cut",
    )(info, *sources)
    return [flat[2 * i : 2 * i + 2] for i in range(len(parts))]


def fetch(p, after=None):
    if after is not None:
        p, _ = lax.optimization_barrier((p, after))
    return send(p[0], X1), send(p[1], X3)


def swap(ab, after=None):
    if after is not None:
        ab, _ = lax.optimization_barrier((ab, after))
    return *ab, send(ab[0], CORE), send(ab[1], CORE)


def fill(info, quarters, at, n, dst, base, sems, first):
    width = dst.shape[1]
    copies = []
    for j, ref in enumerate(quarters):
        who = info[0] if j < 2 else 1 - info[0]
        row = pl.multiple_of(base + who * (2 * n) + (j % 2) * n, 16)
        c = pltpu.make_async_copy(
            ref.at[pl.ds(at, n), pl.ds(0, width)], dst.at[pl.ds(row, n)], sems.at[first + j]
        )
        c.start()
        copies.append(c)
    return copies


def bring(src, dst, sem):
    c = pltpu.make_async_copy(src, dst, sem)
    c.start()
    return c


def wait(copies):
    for c in copies:
        c.wait()


def rms(t, gain):
    scale = lax.rsqrt(jnp.mean(t * t, axis=-1, keepdims=True) + 1e-06)
    return (t * scale * gain).astype(BF)


def dot(a, b):
    return jnp.dot(a, b, preferred_element_type=F32)


def dot_t(a, b):
    return lax.dot_general(a, b, (((1,), (1,)), ((), ())), preferred_element_type=F32)


def head_norm(t):
    return t * lax.rsqrt(jnp.mean(t * t, axis=-1, keepdims=True) + 1e-06)


def open_qkv(l, info, wq, quarters, w, sems):
    return [bring(wq.at[l], w.at[pl.ds(0, D)], sems.at[4])] + fill(
        info, quarters, 0, NQ, w, D, sems, 0
    )


def open_rest(l, info, own, quarters, back, up, down, sems):
    wo, wu, wd = own
    copies = [bring(wo.at[l], back.at[pl.ds(0, S)], sems.at[12])]
    copies += fill(info, quarters, 0, NO, back, S, sems, 0)
    copies += [bring(wu.at[l], up.at[pl.ds(0, D)], sems.at[13])]
    copies += fill(info, quarters, NO, NU, up, D, sems, 4)
    copies += [bring(wd.at[l], down.at[pl.ds(0, D)], sems.at[14])]
    copies += fill(info, quarters, NO + NU, NU, down, D, sems, 8)
    return copies


def scales(info, temps, l, g):
    group = info[2] if g == 0 else 1 - info[2]
    return [temps[l, group * RATIO + r] * QSCALE for r in range(RATIO)]


def project(h, w, ts, q_ref, kv_ref, row, g, keys):
    n = h.shape[0]
    first = 0 if ts is not None else RATIO * HEAD
    last = G if keys else RATIO * HEAD
    raw = dot(h, w[pl.ds(g * D, D), first:last])
    if ts is not None:
        for r in range(RATIO):
            t = head_norm(raw[:, r * HEAD : (r + 1) * HEAD])
            q_ref[pl.ds((g * RATIO + r) * S + row, n), :] = (t * ts[r]).astype(BF)
    if keys:
        at = RATIO * HEAD - first
        kv_ref[pl.ds(row, n), pl.ds(g * 2 * HEAD, HEAD)] = head_norm(
            raw[:, at : at + HEAD]
        ).astype(BF)
        kv_ref[pl.ds(row, n), pl.ds(g * 2 * HEAD + HEAD, HEAD)] = raw[:, at + HEAD :].astype(BF)


QKV_STEP = 192
MIX_STEP = 384
END_STEP = 192
WQ = jax.ShapeDtypeStruct((2 * D, G), BF)
REST = [jax.ShapeDtypeStruct((n * D, D), BF) for n in (1, 2, 2)]
KV = jax.ShapeDtypeStruct((S, 4 * HEAD), BF)
Q = jax.ShapeDtypeStruct((2 * RATIO * S, HEAD), BF)
X = jax.ShapeDtypeStruct((S, D), BF)


def over(n, step, body, loop=False):
    if not loop:
        for row in range(0, n, step):
            body(row)
        return

    @pl.loop(0, n // step)
    def _(i):
        body(pl.multiple_of(i * step, step))


def norm_all(l, x_ref, gain, h):
    def one(row):
        rows = pl.ds(row, QKV_STEP)
        h[rows, :] = rms(x_ref[rows, :].astype(F32), gain[pl.ds(l, 1), :])

    over(S, QKV_STEP, one)


def all_project(l, info, temps, h, w, q_ref, kv_ref, g):
    ts = None if q_ref is None else scales(info, temps, l, g)

    def one(row):
        project(h[pl.ds(row, QKV_STEP), :], w, ts, q_ref, kv_ref, row, g, kv_ref is not None)

    over(S, QKV_STEP, one)


def call(body, outs, ins, flops, scratch=(), mib=16):
    return pl.pallas_call(
        body,
        out_shape=outs,
        in_specs=[spec for spec, _ in ins],
        out_specs=[VMEM] * len(outs),
        scratch_shapes=list(scratch),
        compiler_params=params(mib),
        cost_estimate=cost(flops, 8 << 20),
    )(*[v for _, v in ins])


def qkv_kernel(l, info, temps, x_ref, gain, wq, a, b, d, e, q_ref, kv_ref, w, h, sems):
    copies = open_qkv(l, info, wq, (a, b, d, e), w, sems)
    norm_all(l, x_ref, gain, h)
    copies[0].wait()
    all_project(l, info, temps, h, w, q_ref, kv_ref, 0)
    wait(copies[1:])
    all_project(l, info, temps, h, w, q_ref, kv_ref, 1)


def spread_values(kv, at, ext, i):
    ext[i, :, :HEAD] = kv[:, at + HEAD : at + 2 * HEAD]
    ext[i, :, HEAD:] = jnp.ones((S, HEAD), BF)


def each_head(g, body, loop):
    def one(h):
        for row in range(0, S, MIX_STEP):
            body(
                pl.ds(pl.multiple_of(h * S + row, MIX_STEP), MIX_STEP),
                pl.ds(row, MIX_STEP),
                pl.ds(pl.multiple_of(h * HEAD, HEAD), HEAD),
            )

    if loop:
        pl.loop(g * RATIO, (g + 1) * RATIO)(one)
    else:
        for h in range(g * RATIO, (g + 1) * RATIO):
            one(h)


def soften(q, kvs, columns, shuts, ext, old=None):
    scores = [dot_t(q, kv[:, at : at + HEAD]) for kv, at in zip(kvs, columns)]
    top = None if old is None else old[1]
    for s, shut in zip(scores, shuts):
        t = s.max(axis=-1, keepdims=True)
        t = t if shut is None else t - shut
        top = t if top is None else jnp.maximum(top, t)
    acc = None if old is None else old[0] * jnp.exp2(old[1] - top)
    for i, (s, shut) in enumerate(zip(scores, shuts)):
        base = top if shut is None else top + shut
        part = dot(jnp.exp2(s - base).astype(BF), ext[i])
        acc = part if acc is None else acc + part
    return acc, top


def close(acc):
    return (acc[:, :HEAD] / acc[:, HEAD:]).astype(BF)


def mix(q_ref, kvs, columns, shuts, o_ref, ext, g):
    for i, (kv, at) in enumerate(zip(kvs, columns)):
        spread_values(kv, at, ext, i)

    def one(rows, to, lanes):
        acc, _ = soften(q_ref[rows, :], kvs, columns, shuts, ext)
        o_ref[to, lanes] = close(acc)

    each_head(g, one, len(kvs) > 1)


def shut_if(bad):
    return jnp.where(bad, 1e30, 0.0)


def begin_kernel(info, q_ref, kv, prior, acc_ref, top_ref, ext):
    shuts = [None, shut_if(info[1] < 1)]
    for g in range(2):
        columns = (g * 2 * HEAD, (1 - g) * 2 * HEAD)
        for i, (v, at) in enumerate(zip((kv, prior), columns)):
            spread_values(v, at, ext, i)

        def one(rows, to, lanes, columns=columns):
            acc, top = soften(q_ref[rows, :], (kv, prior), columns, shuts, ext)
            acc_ref[rows, :] = acc
            top_ref[rows, :] = jnp.broadcast_to(top, (MIX_STEP, HEAD))

        each_head(g, one, True)


def finish_rows(l, x_ref, o_ref, gain, back, up, down, out):
    def one(row):
        rows = pl.ds(row, END_STEP)
        x = (x_ref[rows, :].astype(F32) + dot(o_ref[rows, :], back[...])).astype(BF)
        h = rms(x.astype(F32), gain[pl.ds(l, 1), :])
        y = x.astype(F32)
        for g in range(2):
            t = jax.nn.gelu(dot(h, up[pl.ds(g * D, D), :]), approximate=True).astype(BF)
            y = y + dot(t, down[pl.ds(g * D, D), :])
        out[rows, :] = y.astype(BF)

    over(S, END_STEP, one, True)


def own_kernel(
    info, temps, first, x_ref, q_ref, acc_ref, top_ref, gain_a, gain_m, wq_ref,
    qa, qb, qd, qe, wo, wu, wd, a, b, d, e, out, kv0, wq0, back, up, down, o, h, ext, sems, more,
):
    joint = open_qkv(0, info, wq_ref, (qa, qb, qd, qe), wq0, more)
    copies = open_rest(0, info, (wo, wu, wd), (a, b, d, e), back, up, down, sems)
    norm_all(0, first, gain_a, h)
    wait(joint)
    shuts = [shut_if(info[1] < 2)]
    for g in range(2):
        all_project(0, info, temps, h, wq0, None, kv0, g)
        at = g * 2 * HEAD
        spread_values(kv0, at, ext, 0)

        def one(rows, to, lanes, at=at):
            old = (acc_ref[rows, :], top_ref[rows, :1])
            acc, _ = soften(q_ref[rows, :], (kv0,), (at,), shuts, ext, old)
            o[to, lanes] = close(acc)

        each_head(g, one, False)
    wait(copies)
    finish_rows(0, x_ref, o, gain_m, back, up, down, out)


def first_kernel(
    info, temps, first, kv0, gain_a, gain_m, wq0, back, up, down, wq1,
    kv_out, q, o, x, h, ext,
):
    norm_all(0, first, gain_a, h)
    for g in range(2):
        all_project(0, info, temps, h, wq0, q, None, g)
        mix(q, (kv0,), (g * 2 * HEAD,), [None], o, ext, g)
    finish_rows(0, first, o, gain_m, back, up, down, x)
    norm_all(1, x, gain_a, h)
    for g in range(2):
        all_project(1, info, temps, h, wq1, None, kv_out, g)


def last_kernel(
    info, x_ref, q_ref, kv, prior, kv0, gain_m, wo, wu, wd, a, b, d, e,
    out, back, up, down, o, ext, sems,
):
    copies = open_rest(1, info, (wo, wu, wd), (a, b, d, e), back, up, down, sems)
    shuts = [None, shut_if(info[1] < 1), shut_if(info[1] < 2)]
    for g in range(2):
        mine, theirs = g * 2 * HEAD, (1 - g) * 2 * HEAD
        mix(q_ref, (kv, prior, kv0), (mine, theirs, mine), shuts, o, ext, g)
    wait(copies)
    finish_rows(1, x_ref, o, gain_m, back, up, down, out)


def ext_scratch(n):
    return pltpu.VMEM((n, S, 2 * HEAD), BF)


def program(x, gain_a, wqkv, temps, wout, gain_m, wup, wdown):
    me = lax.axis_index(BOTH)
    info = jnp.stack([(me >> 1) & 1, me, me & 1]).astype(jnp.int32)
    x = x[0]
    own = (wout, wup, wdown)
    own_in = [(HBM, w) for w in own]
    sems = pltpu.SemaphoreType.DMA((15,))
    head = [(SMEM, info), (SMEM, temps)]

    def joint(l, x, quarters):
        return call(
            functools.partial(qkv_kernel, l),
            [Q, KV, WQ] if l else [Q, KV],
            head + [(VMEM, x), (VMEM, gain_a), (HBM, wqkv)] + [(HBM, w) for w in quarters],
            4 * S * D * G,
            ([] if l else [pltpu.VMEM(WQ.shape, BF)]) + [pltpu.VMEM((S, D), BF), sems],
            16 if l else 48,
        )

    parts = []
    for l in range(2):
        parts += [[(0, l, NQ)], [(1, l, NO), (2, l, NU), (3, l, NU)]]
    p = cut(info, (wqkv, *own), parts)
    first, q, kv, prior, q0, r0, q1 = spread_first(x, p, joint)
    r0 = swap(r0)
    acc, top = call(
        begin_kernel,
        [jax.ShapeDtypeStruct((2 * RATIO * S, w), F32) for w in (2 * HEAD, HEAD)],
        [(SMEM, info), (VMEM, q), (VMEM, kv), (VMEM, prior)],
        8 * S * S * D,
        [ext_scratch(2)],
    )
    r1 = fetch(p[3], first)
    gains = [(VMEM, gain_a), (VMEM, gain_m)]
    x, kv0, wq, back, up, down = call(
        own_kernel,
        [X, KV, WQ] + REST,
        head
        + [(VMEM, v) for v in (first, x, q, acc, top)]
        + gains
        + [(HBM, wqkv)]
        + [(HBM, w) for w in q0]
        + own_in
        + [(HBM, w) for w in r0],
        14 * S * D * D + 4 * S * S * D,
        [pltpu.VMEM((S, D), BF)] * 2 + [ext_scratch(1), sems, pltpu.SemaphoreType.DMA((5,))],
    )
    q, kv, wq1 = joint(1, x, swap(q1, acc))
    prior = send(kv, NEXT)
    weights = [(VMEM, w) for w in (wq, back, up, down)]
    r1 = swap(r1, kv)
    (kv0,) = call(
        first_kernel,
        [KV],
        head
        + [(VMEM, first), (VMEM, kv0)]
        + gains
        + weights
        + [(VMEM, wq1)],
        14 * S * D * D + 4 * S * S * D,
        [pltpu.VMEM(Q.shape, BF)] + [pltpu.VMEM((S, D), BF)] * 3 + [ext_scratch(1)],
    )
    (x,) = call(
        last_kernel,
        [X],
        [(SMEM, info)]
        + [(VMEM, v) for v in (x, q, kv, prior, kv0, gain_m)]
        + own_in
        + [(HBM, w) for w in r1],
        10 * S * D * D + 12 * S * S * D,
        [pltpu.VMEM(w.shape, BF) for w in REST] + [pltpu.VMEM((S, D), BF), ext_scratch(3), sems],
    )
    return x[None]


def solution(mesh):
    in_specs = (
        P(BOTH, None, None),
        P(),
        P(None, None, "mp"),
        P(),
        P(None, "mp", None),
        P(),
        P(None, None, "mp"),
        P(None, "mp", None),
    )
    return jax.shard_map(
        program, mesh=mesh, in_specs=in_specs, out_specs=P(BOTH, None, None), check_vma=False
    )
```

profile of v0, /device:TPU:8, one launch (start us, length us, event | category | flops | bytes accessed | tf_op | source)
XLA Modules:
  0.0 161.6 jit_solution(16595850751936366341)
XLA Ops:
  0.0 1.7 %slice.33 = bf16[384,384]{1,0:T(8,128)(2,1)} slice(bf16[384,768]{1,0:T(8,128)(2,1)} %bitcast.5), slice={[0:384], [384:768]} | slice | bytes 589824 | tf_op jit(solution)/shard_map/slice | solution.py:56
  2.4 4.5 %cut.1 = (bf16[192,640]{1,0:T(8,128)(2,1)}, bf16[192,640]{1,0:T(8,128)(2,1)}, bf16[480,768]{1,0:T(8,128)(2,1)}, bf16[480,768]{1,0:T(8,128)(2,1)}, bf16[192,640]{...) custom-call(s32[3]{0:T(128)} %pad_add_fusion.info, ...), custom_call_target="tpu_custom_call" | custom-call | tf_op jit(solution)/shard_map/cut/pallas_call | solution.py:139
  6.9 1.7 %collective-permute-start.1 = (bf16[192,384]{1,0:T(8,128)(2,1)S(1)}, bf16[192,384]{1,0:T(8,128)(2,1)S(1)}, u32[]{:S(2)}, u32[]{:S(2)}) collective-permute-start(bf16[192,384]{1,0:T(8,128)(2,1)S(1)} %slice.27), channel_id=1, source_target_pairs={{0,12},{1,13},{2,14},{3,15},{4,8},{5,9},{6,10},{7,11},{8,4},{9,5},... | collective-permute-start | bytes 442376 | tf_op jit(solution)/shard_map/ppermute | solution.py:48
  8.6 4.7 %collective-permute-done.1 = bf16[192,384]{1,0:T(8,128)(2,1)S(1)} collective-permute-done((bf16[192,384]{1,0:T(8,128)(2,1)S(1)}, bf16[192,384]{1,0:T(8,128)(2,1)S(1)}, u32[]{:S(2)}, u32[]{:S(2)}) %collective-permute-start.1) | collective-permute-done | bytes 147488 | tf_op jit(solution)/shard_map/ppermute | solution.py:48
  13.3 3.5 %collective-permute-start.2 = (bf16[96,384]{1,0:T(8,128)(2,1)S(1)}, bf16[96,384]{1,0:T(8,128)(2,1)S(1)}, u32[]{:S(2)}, u32[]{:S(2)}) collective-permute-start(bf16[96,384]{1,0:T(8,128)(2,1)S(1)} %slice.35), channel_id=1, source_target_pairs={{0,4},{1,5},{2,6},{3,7},{4,0},{5,1},{6,2},{7,3},{8,12},{9,13},{10,... | collective-permute-start | bytes 221192 | tf_op jit(solution)/shard_map/ppermute | solution.py:48
  16.8 1.9 %collective-permute-start.4 = (bf16[192,640]{1,0:T(8,128)(2,1)}, bf16[192,640]{1,0:T(8,128)(2,1)S(1)}, u32[]{:S(2)}, u32[]{:S(2)}) collective-permute-start(bf16[192,640]{1,0:T(8,128)(2,1)} %get-tuple-element.63), channel_id=1, source_target_pairs={{0,129},{1,128},{2,131},{3,130},{4,133},{5,132},{6,135},{7,134},{8... | collective-permute-start | bytes 737288 | tf_op jit(solution)/shard_map/ppermute | solution.py:48
  19.1 5.1 %collective-permute-done.3.a.qa = bf16[192,640]{1,0:T(8,128)(2,1)S(1)} collective-permute-done((bf16[192,640]{1,0:T(8,128)(2,1)}, bf16[192,640]{1,0:T(8,128)(2,1)S(1)}, u32[]{:S(2)}, u32[]{:S(2)}) %collective-permute-start.3) | collective-permute-done | bytes 245792 | tf_op jit(solution)/shard_map/ppermute | solution.py:48
  27.0 2.4 %collective-permute-done.5 = bf16[48,384]{1,0:T(8,128)(2,1)S(1)} collective-permute-done((bf16[48,384]{1,0:T(8,128)(2,1)S(1)}, bf16[48,384]{1,0:T(8,128)(2,1)S(1)}, u32[]{:S(2)}, u32[]{:S(2)}) %collective-permute-start.5) | collective-permute-done | bytes 36896 | tf_op jit(solution)/shard_map/ppermute | solution.py:48
  30.6 2.9 %collective-permute-done.6 = bf16[48,384]{1,0:T(8,128)(2,1)S(1)} collective-permute-done((bf16[48,384]{1,0:T(8,128)(2,1)S(1)}, bf16[48,384]{1,0:T(8,128)(2,1)S(1)}, u32[]{:S(2)}, u32[]{:S(2)}) %collective-permute-start.6) | collective-permute-done | bytes 36896 | tf_op jit(solution)/shard_map/ppermute | solution.py:48
  33.5 1.8 %collective-permute-start.9 = (bf16[48,384]{1,0:T(8,128)(2,1)S(1)}, bf16[48,384]{1,0:T(8,128)(2,1)S(1)}, u32[]{:S(2)}, u32[]{:S(2)}) collective-permute-start(bf16[48,384]{1,0:T(8,128)(2,1)S(1)} %broadcast_select_fusion), channel_id=1, source_target_pairs={{0,129},{1,128},{2,131},{3,130},{4,133},{5,132},{6,135},{7,134},{8... | collective-permute-start | bytes 110600 | tf_op jit(solution)/shard_map/ppermute | solution.py:48
  35.3 3.6 %shard_map.82 = (bf16[2304,128]{1,0:T(8,128)(2,1)S(1)}, bf16[384,512]{1,0:T(8,128)(2,1)S(1)}) custom-call(s32[3]{0:T(128)S(1)} %copy-done.9, f32[2,6]{1,0:T(2,128)S(1)} %copy-done.10, bf16[384,768]{1,0:T(8,128)(2,1)S(1)} %bitcast.7, f32[2,768]{1,0:T(2,128)S(1)} %copy-done.8, bf16[2,768,640]{2,1,0:T(8,128)(2,1)S(1)} %copy-done, ...), custom_call_target="tpu_custom_call" | custom-call | flops 754974720 | bytes 8388608 | tf_op jit(solution)/shard_map/pallas_call | solution.py:284
  40.5 3.4 %collective-permute-start.10 = (bf16[48,384]{1,0:T(8,128)(2,1)S(1)}, bf16[48,384]{1,0:T(8,128)(2,1)S(1)}, u32[]{:S(2)}, u32[]{:S(2)}) collective-permute-start(bf16[48,384]{1,0:T(8,128)(2,1)S(1)} %broadcast_select_fusion.1), channel_id=1, source_target_pairs={{0,32},{1,33},{2,34},{3,35},{4,36},{5,37},{6,38},{7,39},{8,40},{9,... | collective-permute-start | bytes 110600 | tf_op jit(solution)/shard_map/ppermute | solution.py:48
  43.9 4.5 %collective-permute-start.11 = (bf16[48,384]{1,0:T(8,128)(2,1)S(1)}, bf16[48,384]{1,0:T(8,128)(2,1)S(1)}, u32[]{:S(2)}, u32[]{:S(2)}) collective-permute-start(bf16[48,384]{1,0:T(8,128)(2,1)S(1)} %broadcast_select_fusion.1), channel_id=1, source_target_pairs={{0,96},{1,97},{2,98},{3,99},{4,100},{5,101},{6,102},{7,103},{8,104... | collective-permute-start | bytes 110600 | tf_op jit(solution)/shard_map/ppermute | solution.py:48
  48.4 2.0 %collective-permute-done.11 = bf16[48,384]{1,0:T(8,128)(2,1)S(1)} collective-permute-done((bf16[48,384]{1,0:T(8,128)(2,1)S(1)}, bf16[48,384]{1,0:T(8,128)(2,1)S(1)}, u32[]{:S(2)}, u32[]{:S(2)}) %collective-permute-start.11) | collective-permute-done | bytes 36896 | tf_op jit(solution)/shard_map/ppermute | solution.py:48
  50.4 4.2 %collective-permute-start.12 = (bf16[48,384]{1,0:T(8,128)(2,1)S(1)}, bf16[48,384]{1,0:T(8,128)(2,1)S(1)}, u32[]{:S(2)}, u32[]{:S(2)}) collective-permute-start(bf16[48,384]{1,0:T(8,128)(2,1)S(1)} %select_select_fusion), channel_id=1, source_target_pairs={{0,96},{1,97},{2,98},{3,99},{4,100},{5,101},{6,102},{7,103},{8,104... | collective-permute-start | bytes 110600 | tf_op jit(solution)/shard_map/ppermute | solution.py:48
  56.5 1.9 %collective-permute-start.13 = (bf16[48,384]{1,0:T(8,128)(2,1)S(1)}, bf16[48,384]{1,0:T(8,128)(2,1)S(1)}, u32[]{:S(2)}, u32[]{:S(2)}) collective-permute-start(bf16[48,384]{1,0:T(8,128)(2,1)S(1)} %broadcast_select_fusion.2), channel_id=1, source_target_pairs={{0,16},{1,17},{2,18},{3,19},{4,20},{5,21},{6,22},{7,23},{8,24},{9,... | collective-permute-start | bytes 110600 | tf_op jit(solution)/shard_map/ppermute | solution.py:48
  58.5 2.1 %collective-permute-done.13 = bf16[48,384]{1,0:T(8,128)(2,1)S(1)} collective-permute-done((bf16[48,384]{1,0:T(8,128)(2,1)S(1)}, bf16[48,384]{1,0:T(8,128)(2,1)S(1)}, u32[]{:S(2)}, u32[]{:S(2)}) %collective-permute-start.13) | collective-permute-done | bytes 36896 | tf_op jit(solution)/shard_map/ppermute | solution.py:48
  61.1 4.0 %collective-permute-done.14 = bf16[96,384]{1,0:T(8,128)(2,1)S(1)} collective-permute-done((bf16[96,384]{1,0:T(8,128)(2,1)S(1)}, bf16[96,384]{1,0:T(8,128)(2,1)S(1)}, u32[]{:S(2)}, u32[]{:S(2)}) %collective-permute-start.14) | collective-permute-done | bytes 73760 | tf_op jit(solution)/shard_map/ppermute | solution.py:48
  65.0 2.4 %collective-permute-start.15 = (bf16[192,384]{1,0:T(8,128)(2,1)S(1)}, bf16[192,384]{1,0:T(8,128)(2,1)S(1)}, u32[]{:S(2)}, u32[]{:S(2)}) collective-permute-start(bf16[192,384]{1,0:T(8,128)(2,1)S(1)} %pad_maximum_fusion.1), channel_id=1, source_target_pairs={{0,12},{1,13},{2,14},{3,15},{4,8},{5,9},{6,10},{7,11},{8,4},{9,5},... | collective-permute-start | bytes 442376 | tf_op jit(solution)/shard_map/ppermute | solution.py:48
  67.4 3.1 %collective-permute-done.15 = bf16[192,384]{1,0:T(8,128)(2,1)S(1)} collective-permute-done((bf16[192,384]{1,0:T(8,128)(2,1)S(1)}, bf16[192,384]{1,0:T(8,128)(2,1)S(1)}, u32[]{:S(2)}, u32[]{:S(2)}) %collective-permute-start.15) | collective-permute-done | bytes 147488 | tf_op jit(solution)/shard_map/ppermute | solution.py:48
  71.6 2.4 %collective-permute-start.17 = (bf16[384,512]{1,0:T(8,128)(2,1)}, bf16[384,512]{1,0:T(8,128)(2,1)S(1)}, u32[]{:S(2)}, u32[]{:S(2)}) collective-permute-start(bf16[384,512]{1,0:T(8,128)(2,1)} %copy-done.12), channel_id=1, source_target_pairs={{0,1},{1,2},{2,3},{3,4},{4,5},{5,6},{6,7},{7,8},{8,9},{9,10},{10,1... | collective-permute-start | bytes 1179656 | tf_op jit(solution)/shard_map/ppermute | solution.py:48
  74.0 1.8 %collective-permute-start.22 = (bf16[192,640]{1,0:T(8,128)(2,1)}, bf16[192,640]{1,0:T(8,128)(2,1)S(1)}, u32[]{:S(2)}, u32[]{:S(2)}) collective-permute-start(bf16[192,640]{1,0:T(8,128)(2,1)} %get-tuple-element.85), channel_id=1, source_target_pairs={{0,1},{1,0},{2,3},{3,2},{4,5},{5,4},{6,7},{7,6},{8,9},{9,8},{10,11... | collective-permute-start | bytes 737288 | tf_op jit(solution)/shard_map/ppermute | solution.py:48
  76.3 13.7 %collective-permute-done.22.a = bf16[192,640]{1,0:T(8,128)(2,1)S(1)} collective-permute-done((bf16[192,640]{1,0:T(8,128)(2,1)}, bf16[192,640]{1,0:T(8,128)(2,1)S(1)}, u32[]{:S(2)}, u32[]{:S(2)}) %collective-permute-start.22) | collective-permute-done | bytes 245792 | tf_op jit(solution)/shard_map/ppermute | solution.py:48
  90.0 2.1 %collective-permute-start.28 = (bf16[480,768]{1,0:T(8,128)(2,1)}, bf16[480,768]{1,0:T(8,128)(2,1)S(1)}, u32[]{:S(2)}, u32[]{:S(2)}) collective-permute-start(bf16[480,768]{1,0:T(8,128)(2,1)} %get-tuple-element.98), channel_id=1, source_target_pairs={{0,129},{1,128},{2,131},{3,130},{4,133},{5,132},{6,135},{7,134},{8... | collective-permute-start | bytes 2211848 | tf_op jit(solution)/shard_map/ppermute | solution.py:48
  94.3 6.0 %shard_map.83 = (f32[2304,256]{1,0:T(8,128)S(1)}, f32[2304,128]{1,0:T(8,128)S(1)}) custom-call(s32[3]{0:T(128)S(1)} %copy-done.9, bf16[2304,128]{1,0:T(8,128)(2,1)S(1)} %copy-done.7, bf16[384,512]{1,0:T(8,128)(2,1)S(1)} %copy-done.13, bf16[384,512]{1,0:T(8,128)(2,1)S(1)} %collective-permute-done.17.prior), custom_call_target="tpu_custom_call" | custom-call | flops 905969664 | bytes 8388608 | tf_op jit(solution)/shard_map/pallas_call | solution.py:284
  100.2 14.6 %collective-permute-done.23.b = bf16[192,640]{1,0:T(8,128)(2,1)S(1)} collective-permute-done((bf16[192,640]{1,0:T(8,128)(2,1)}, bf16[192,640]{1,0:T(8,128)(2,1)S(1)}, u32[]{:S(2)}, u32[]{:S(2)}) %collective-permute-start.23) | collective-permute-done | bytes 245792 | tf_op jit(solution)/shard_map/ppermute | solution.py:48
  117.2 11.4 %shard_map.84 = (bf16[384,768]{1,0:T(8,128)(2,1)S(1)}, bf16[384,512]{1,0:T(8,128)(2,1)S(1)}, bf16[1536,640]{1,0:T(8,128)(2,1)S(1)}, bf16[768,768]{1,0:T(8,128)(2...) custom-call(s32[3]{0:T(128)S(1)} %copy-done.9, f32[2,6]{1,0:T(2,128)S(1)} %copy-done.10, ...), custom_call_target="tpu_custom_call" | custom-call | flops 3623878656 | bytes 8388608 | tf_op jit(solution)/shard_map/pallas_call | solution.py:284
  128.6 3.9 %shard_map.85 = (bf16[2304,128]{1,0:T(8,128)(2,1)S(1)}, bf16[384,512]{1,0:T(8,128)(2,1)S(1)}, bf16[1536,640]{1,0:T(8,128)(2,1)S(1)}) custom-call(s32[3]{0:T(128)S(1)} %copy-done.9, f32[2,6]{1,0:T(2,128)S(1)} %copy-done.10, bf16[384,768]{1,0:T(8,128)(2,1)S(1)} %get-tuple-element.82.x_ref, f32[2,768]{1,0:T(2,128)S(1)} %copy-done.8, ...), custom_call_target="tpu_custom_call" | custom-call | flops 754974720 | bytes 8388608 | tf_op jit(solution)/shard_map/pallas_call | solution.py:284
  133.2 2.7 %collective-permute-start.26 = (bf16[384,512]{1,0:T(8,128)(2,1)S(1)}, bf16[384,512]{1,0:T(8,128)(2,1)S(1)}, u32[]{:S(2)}, u32[]{:S(2)}) collective-permute-start(bf16[384,512]{1,0:T(8,128)(2,1)S(1)} %get-tuple-element.90.kv), channel_id=1, source_target_pairs={{0,1},{1,2},{2,3},{3,4},{4,5},{5,6},{6,7},{7,8},{8,9},{9,10},{10,1... | collective-permute-start | bytes 1179656 | tf_op jit(solution)/shard_map/ppermute | solution.py:48
  135.9 7.9 %shard_map.86.kv0 = bf16[384,512]{1,0:T(8,128)(2,1)S(1)} custom-call(s32[3]{0:T(128)S(1)} %copy-done.9, f32[2,6]{1,0:T(2,128)S(1)} %copy-done.10, bf16[384,768]{1,0:T(8,128)(2,1)S(1)} %maximum_select_fusion.first, bf16[384,512]{1,0:T(8,128)(2,1)S(1)} %get-tuple-element.91.kv0, f32[2,768]{1,0:T(2,128)S(1)} %copy-done.8, f32[2,768]{1,0:T(2,128)S(1)} %copy-done.11, ...), custom_call_target="tpu_custom_call" | custom-call | flops 3623878656 | bytes 8388608 | tf_op jit(solution)/shard_map/pallas_call | solution.py:284
  143.8 3.5 %collective-permute-done.26.prior = bf16[384,512]{1,0:T(8,128)(2,1)S(1)} collective-permute-done((bf16[384,512]{1,0:T(8,128)(2,1)S(1)}, bf16[384,512]{1,0:T(8,128)(2,1)S(1)}, u32[]{:S(2)}, u32[]{:S(2)}) %collective-permute-start.26) | collective-permute-done | bytes 393248 | tf_op jit(solution)/shard_map/ppermute | solution.py:48
  147.4 14.1 %shard_map.87 = bf16[384,768]{1,0:T(8,128)(2,1)} custom-call(s32[3]{0:T(128)S(1)} %copy-done.9, bf16[384,768]{1,0:T(8,128)(2,1)S(1)} %get-tuple-element.82.x_ref, bf16[2304,128]{1,0:T(8,128)(2,1)S(1)} %get-tuple-element.89.q_ref, bf16[384,512]{1,0:T(8,128)(2,1)S(1)} %get-tuple-element.90.kv, bf16[384,512]{1,0:T(8,128)(2,1)S(1)} %collective-permute-done.26.prior, ...), custom_call_target="tpu_custom_call" | custom-call | flops 3623878656 | bytes 8388608 | tf_op jit(solution)/shard_map/pallas_call | solution.py:284
  (82 shorter events, 16.0 us)
Async XLA Ops:
  1.7 5.2 %collective-permute-start = (bf16[384,384]{1,0:T(8,128)(2,1)}, bf16[384,384]{1,0:T(8,128)(2,1)S(1)}, u32[]{:S(2)}, u32[]{:S(2)}) collective-permute-start(bf16[384,384]{1,0:T(8,128)(2,1)} %slice.33), channel_id=1, source_target_pairs={{0,2},{1,3},{2,0},{3,1},{4,6},{5,7},{6,4},{7,5},{8,10},{9,11},{10,... | collective-permute-start | bytes 884744 | tf_op jit(solution)/shard_map/ppermute | solution.py:48
  6.9 6.3 %collective-permute-start.1 = (bf16[192,384]{1,0:T(8,128)(2,1)S(1)}, bf16[192,384]{1,0:T(8,128)(2,1)S(1)}, u32[]{:S(2)}, u32[]{:S(2)}) collective-permute-start(bf16[192,384]{1,0:T(8,128)(2,1)S(1)} %slice.27), channel_id=1, source_target_pairs={{0,12},{1,13},{2,14},{3,15},{4,8},{5,9},{6,10},{7,11},{8,4},{9,5},... | collective-permute-start | bytes 442376 | tf_op jit(solution)/shard_map/ppermute | solution.py:48
  13.3 5.8 %collective-permute-start.2 = (bf16[96,384]{1,0:T(8,128)(2,1)S(1)}, bf16[96,384]{1,0:T(8,128)(2,1)S(1)}, u32[]{:S(2)}, u32[]{:S(2)}) collective-permute-start(bf16[96,384]{1,0:T(8,128)(2,1)S(1)} %slice.35), channel_id=1, source_target_pairs={{0,4},{1,5},{2,6},{3,7},{4,0},{5,1},{6,2},{7,3},{8,12},{9,13},{10,... | collective-permute-start | bytes 221192 | tf_op jit(solution)/shard_map/ppermute | solution.py:48
  16.8 7.4 %collective-permute-start.3 = (bf16[192,640]{1,0:T(8,128)(2,1)}, bf16[192,640]{1,0:T(8,128)(2,1)S(1)}, u32[]{:S(2)}, u32[]{:S(2)}) collective-permute-start(bf16[192,640]{1,0:T(8,128)(2,1)} %get-tuple-element.62), channel_id=1, source_target_pairs={{0,1},{1,0},{2,3},{3,2},{4,5},{5,4},{6,7},{7,6},{8,9},{9,8},{10,11... | collective-permute-start | bytes 737288 | tf_op jit(solution)/shard_map/ppermute | solution.py:48
  16.8 8.7 %collective-permute-start.4 = (bf16[192,640]{1,0:T(8,128)(2,1)}, bf16[192,640]{1,0:T(8,128)(2,1)S(1)}, u32[]{:S(2)}, u32[]{:S(2)}) collective-permute-start(bf16[192,640]{1,0:T(8,128)(2,1)} %get-tuple-element.63), channel_id=1, source_target_pairs={{0,129},{1,128},{2,131},{3,130},{4,133},{5,132},{6,135},{7,134},{8... | collective-permute-start | bytes 737288 | tf_op jit(solution)/shard_map/ppermute | solution.py:48
  25.4 4.0 %collective-permute-start.5 = (bf16[48,384]{1,0:T(8,128)(2,1)S(1)}, bf16[48,384]{1,0:T(8,128)(2,1)S(1)}, u32[]{:S(2)}, u32[]{:S(2)}) collective-permute-start(bf16[48,384]{1,0:T(8,128)(2,1)S(1)} %slice.31), channel_id=1, source_target_pairs={{0,16},{1,17},{2,18},{3,19},{4,20},{5,21},{6,22},{7,23},{8,24},{9,... | collective-permute-start | bytes 110600 | tf_op jit(solution)/shard_map/ppermute | solution.py:48
  29.4 4.0 %collective-permute-start.6 = (bf16[48,384]{1,0:T(8,128)(2,1)S(1)}, bf16[48,384]{1,0:T(8,128)(2,1)S(1)}, u32[]{:S(2)}, u32[]{:S(2)}) collective-permute-start(bf16[48,384]{1,0:T(8,128)(2,1)S(1)} %slice_select_fusion.3), channel_id=1, source_target_pairs={{0,1},{1,0},{2,3},{3,2},{4,5},{5,4},{6,7},{7,6},{8,9},{9,8},{10,11... | collective-permute-start | bytes 110600 | tf_op jit(solution)/shard_map/ppermute | solution.py:48
  30.0 3.4 %collective-permute-start.7 = (bf16[192,640]{1,0:T(8,128)(2,1)S(1)}, bf16[192,640]{1,0:T(8,128)(2,1)S(1)}, u32[]{:S(2)}, u32[]{:S(2)}) collective-permute-start(bf16[192,640]{1,0:T(8,128)(2,1)S(1)} %collective-permute-done.3.a.qa), channel_id=1, source_target_pairs={{0,2},{1,3},{2,0},{3,1},{4,6},{5,7},{6,4},{7,5},{8,10},{9,11},{10,... | collective-permute-start | bytes 737288 | tf_op jit(solution)/shard_map/ppermute | solution.py:48
  30.0 3.4 %collective-permute-start.8 = (bf16[192,640]{1,0:T(8,128)(2,1)S(1)}, bf16[192,640]{1,0:T(8,128)(2,1)}, u32[]{:S(2)}, u32[]{:S(2)}) collective-permute-start(bf16[192,640]{1,0:T(8,128)(2,1)S(1)} %collective-permute-done.4.b.qb), channel_id=1, source_target_pairs={{0,2},{1,3},{2,0},{3,1},{4,6},{5,7},{6,4},{7,5},{8,10},{9,11},{10,... | collective-permute-start | bytes 737288 | tf_op jit(solution)/shard_map/ppermute | solution.py:48
  33.5 7.0 %collective-permute-start.9 = (bf16[48,384]{1,0:T(8,128)(2,1)S(1)}, bf16[48,384]{1,0:T(8,128)(2,1)S(1)}, u32[]{:S(2)}, u32[]{:S(2)}) collective-permute-start(bf16[48,384]{1,0:T(8,128)(2,1)S(1)} %broadcast_select_fusion), channel_id=1, source_target_pairs={{0,129},{1,128},{2,131},{3,130},{4,133},{5,132},{6,135},{7,134},{8... | collective-permute-start | bytes 110600 | tf_op jit(solution)/shard_map/ppermute | solution.py:48
  40.5 7.8 %collective-permute-start.10 = (bf16[48,384]{1,0:T(8,128)(2,1)S(1)}, bf16[48,384]{1,0:T(8,128)(2,1)S(1)}, u32[]{:S(2)}, u32[]{:S(2)}) collective-permute-start(bf16[48,384]{1,0:T(8,128)(2,1)S(1)} %broadcast_select_fusion.1), channel_id=1, source_target_pairs={{0,32},{1,33},{2,34},{3,35},{4,36},{5,37},{6,38},{7,39},{8,40},{9,... | collective-permute-start | bytes 110600 | tf_op jit(solution)/shard_map/ppermute | solution.py:48
  43.9 6.4 %collective-permute-start.11 = (bf16[48,384]{1,0:T(8,128)(2,1)S(1)}, bf16[48,384]{1,0:T(8,128)(2,1)S(1)}, u32[]{:S(2)}, u32[]{:S(2)}) collective-permute-start(bf16[48,384]{1,0:T(8,128)(2,1)S(1)} %broadcast_select_fusion.1), channel_id=1, source_target_pairs={{0,96},{1,97},{2,98},{3,99},{4,100},{5,101},{6,102},{7,103},{8,104... | collective-permute-start | bytes 110600 | tf_op jit(solution)/shard_map/ppermute | solution.py:48
  50.4 6.2 %collective-permute-start.12 = (bf16[48,384]{1,0:T(8,128)(2,1)S(1)}, bf16[48,384]{1,0:T(8,128)(2,1)S(1)}, u32[]{:S(2)}, u32[]{:S(2)}) collective-permute-start(bf16[48,384]{1,0:T(8,128)(2,1)S(1)} %select_select_fusion), channel_id=1, source_target_pairs={{0,96},{1,97},{2,98},{3,99},{4,100},{5,101},{6,102},{7,103},{8,104... | collective-permute-start | bytes 110600 | tf_op jit(solution)/shard_map/ppermute | solution.py:48
  54.5 16.3 %collective-permute-start.18 = (bf16[480,768]{1,0:T(8,128)(2,1)}, bf16[480,768]{1,0:T(8,128)(2,1)S(1)}, u32[]{:S(2)}, u32[]{:S(2)}) collective-permute-start(bf16[480,768]{1,0:T(8,128)(2,1)} %get-tuple-element.80), channel_id=1, source_target_pairs={{0,1},{1,0},{2,3},{3,2},{4,5},{5,4},{6,7},{7,6},{8,9},{9,8},{10,11... | collective-permute-start | bytes 2211848 | tf_op jit(solution)/shard_map/ppermute | solution.py:48
  54.6 17.0 %collective-permute-start.19 = (bf16[480,768]{1,0:T(8,128)(2,1)}, bf16[480,768]{1,0:T(8,128)(2,1)S(1)}, u32[]{:S(2)}, u32[]{:S(2)}) collective-permute-start(bf16[480,768]{1,0:T(8,128)(2,1)} %get-tuple-element.81), channel_id=1, source_target_pairs={{0,129},{1,128},{2,131},{3,130},{4,133},{5,132},{6,135},{7,134},{8... | collective-permute-start | bytes 2211848 | tf_op jit(solution)/shard_map/ppermute | solution.py:48
  56.5 4.0 %collective-permute-start.13 = (bf16[48,384]{1,0:T(8,128)(2,1)S(1)}, bf16[48,384]{1,0:T(8,128)(2,1)S(1)}, u32[]{:S(2)}, u32[]{:S(2)}) collective-permute-start(bf16[48,384]{1,0:T(8,128)(2,1)S(1)} %broadcast_select_fusion.2), channel_id=1, source_target_pairs={{0,16},{1,17},{2,18},{3,19},{4,20},{5,21},{6,22},{7,23},{8,24},{9,... | collective-permute-start | bytes 110600 | tf_op jit(solution)/shard_map/ppermute | solution.py:48
  60.6 4.4 %collective-permute-start.14 = (bf16[96,384]{1,0:T(8,128)(2,1)S(1)}, bf16[96,384]{1,0:T(8,128)(2,1)S(1)}, u32[]{:S(2)}, u32[]{:S(2)}) collective-permute-start(bf16[96,384]{1,0:T(8,128)(2,1)S(1)} %pad_maximum_fusion.2), channel_id=1, source_target_pairs={{0,4},{1,5},{2,6},{3,7},{4,0},{5,1},{6,2},{7,3},{8,12},{9,13},{10,... | collective-permute-start | bytes 221192 | tf_op jit(solution)/shard_map/ppermute | solution.py:48
  65.0 5.5 %collective-permute-start.15 = (bf16[192,384]{1,0:T(8,128)(2,1)S(1)}, bf16[192,384]{1,0:T(8,128)(2,1)S(1)}, u32[]{:S(2)}, u32[]{:S(2)}) collective-permute-start(bf16[192,384]{1,0:T(8,128)(2,1)S(1)} %pad_maximum_fusion.1), channel_id=1, source_target_pairs={{0,12},{1,13},{2,14},{3,15},{4,8},{5,9},{6,10},{7,11},{8,4},{9,5},... | collective-permute-start | bytes 442376 | tf_op jit(solution)/shard_map/ppermute | solution.py:48
  70.5 45.4 %copy-start.2 = (bf16[2,768,768]{2,1,0:T(8,128)(2,1)S(1)}, bf16[2,768,768]{2,1,0:T(8,128)(2,1)}, u32[]{:S(2)}) copy-start(bf16[2,768,768]{2,1,0:T(8,128)(2,1)} %wd.3) | copy-start | bytes 7077892
  70.6 5.2 %collective-permute-start.16 = (bf16[384,384]{1,0:T(8,128)(2,1)S(1)}, bf16[384,384]{1,0:T(8,128)(2,1)S(1)}, u32[]{:S(2)}, u32[]{:S(2)}) collective-permute-start(bf16[384,384]{1,0:T(8,128)(2,1)S(1)} %pad_maximum_fusion), channel_id=1, source_target_pairs={{0,2},{1,3},{2,0},{3,1},{4,6},{5,7},{6,4},{7,5},{8,10},{9,11},{10,... | collective-permute-start | bytes 884744 | tf_op jit(solution)/shard_map/ppermute | solution.py:48
  70.9 45.0 %collective-permute-start.20 = (bf16[480,768]{1,0:T(8,128)(2,1)S(1)}, bf16[480,768]{1,0:T(8,128)(2,1)S(1)}, u32[]{:S(2)}, u32[]{:S(2)}) collective-permute-start(bf16[480,768]{1,0:T(8,128)(2,1)S(1)} %collective-permute-done.18.a), channel_id=1, source_target_pairs={{0,2},{1,3},{2,0},{3,1},{4,6},{5,7},{6,4},{7,5},{8,10},{9,11},{10,... | collective-permute-start | bytes 2211848 | tf_op jit(solution)/shard_map/ppermute | solution.py:48
  71.6 44.3 %collective-permute-start.21 = (bf16[480,768]{1,0:T(8,128)(2,1)S(1)}, bf16[480,768]{1,0:T(8,128)(2,1)S(1)}, u32[]{:S(2)}, u32[]{:S(2)}) collective-permute-start(bf16[480,768]{1,0:T(8,128)(2,1)S(1)} %collective-permute-done.19.b), channel_id=1, source_target_pairs={{0,2},{1,3},{2,0},{3,1},{4,6},{5,7},{6,4},{7,5},{8,10},{9,11},{10,... | collective-permute-start | bytes 2211848 | tf_op jit(solution)/shard_map/ppermute | solution.py:48
  71.6 20.5 %collective-permute-start.17 = (bf16[384,512]{1,0:T(8,128)(2,1)}, bf16[384,512]{1,0:T(8,128)(2,1)S(1)}, u32[]{:S(2)}, u32[]{:S(2)}) collective-permute-start(bf16[384,512]{1,0:T(8,128)(2,1)} %copy-done.12), channel_id=1, source_target_pairs={{0,1},{1,2},{2,3},{3,4},{4,5},{5,6},{6,7},{7,8},{8,9},{9,10},{10,1... | collective-permute-start | bytes 1179656 | tf_op jit(solution)/shard_map/ppermute | solution.py:48
  74.0 16.1 %collective-permute-start.22 = (bf16[192,640]{1,0:T(8,128)(2,1)}, bf16[192,640]{1,0:T(8,128)(2,1)S(1)}, u32[]{:S(2)}, u32[]{:S(2)}) collective-permute-start(bf16[192,640]{1,0:T(8,128)(2,1)} %get-tuple-element.85), channel_id=1, source_target_pairs={{0,1},{1,0},{2,3},{3,2},{4,5},{5,4},{6,7},{7,6},{8,9},{9,8},{10,11... | collective-permute-start | bytes 737288 | tf_op jit(solution)/shard_map/ppermute | solution.py:48
  75.9 56.6 %collective-permute-start.27 = (bf16[480,768]{1,0:T(8,128)(2,1)}, bf16[480,768]{1,0:T(8,128)(2,1)S(1)}, u32[]{:S(2)}, u32[]{:S(2)}) collective-permute-start(bf16[480,768]{1,0:T(8,128)(2,1)} %get-tuple-element.97), channel_id=1, source_target_pairs={{0,1},{1,0},{2,3},{3,2},{4,5},{5,4},{6,7},{7,6},{8,9},{9,8},{10,11... | collective-permute-start | bytes 2211848 | tf_op jit(solution)/shard_map/ppermute | solution.py:48
  90.0 42.5 %collective-permute-start.28 = (bf16[480,768]{1,0:T(8,128)(2,1)}, bf16[480,768]{1,0:T(8,128)(2,1)S(1)}, u32[]{:S(2)}, u32[]{:S(2)}) collective-permute-start(bf16[480,768]{1,0:T(8,128)(2,1)} %get-tuple-element.98), channel_id=1, source_target_pairs={{0,129},{1,128},{2,131},{3,130},{4,133},{5,132},{6,135},{7,134},{8... | collective-permute-start | bytes 2211848 | tf_op jit(solution)/shard_map/ppermute | solution.py:48
  92.1 22.8 %collective-permute-start.23 = (bf16[192,640]{1,0:T(8,128)(2,1)}, bf16[192,640]{1,0:T(8,128)(2,1)S(1)}, u32[]{:S(2)}, u32[]{:S(2)}) collective-permute-start(bf16[192,640]{1,0:T(8,128)(2,1)} %get-tuple-element.86), channel_id=1, source_target_pairs={{0,129},{1,128},{2,131},{3,130},{4,133},{5,132},{6,135},{7,134},{8... | collective-permute-start | bytes 737288 | tf_op jit(solution)/shard_map/ppermute | solution.py:48
  114.9 13.7 %collective-permute-start.24 = (bf16[192,640]{1,0:T(8,128)(2,1)S(1)}, bf16[192,640]{1,0:T(8,128)(2,1)S(1)}, u32[]{:S(2)}, u32[]{:S(2)}) collective-permute-start(bf16[192,640]{1,0:T(8,128)(2,1)S(1)} %collective-permute-done.22.a), channel_id=1, source_target_pairs={{0,2},{1,3},{2,0},{3,1},{4,6},{5,7},{6,4},{7,5},{8,10},{9,11},{10,... | collective-permute-start | bytes 737288 | tf_op jit(solution)/shard_map/ppermute | solution.py:48
  115.9 12.7 %collective-permute-start.25 = (bf16[192,640]{1,0:T(8,128)(2,1)S(1)}, bf16[192,640]{1,0:T(8,128)(2,1)S(1)}, u32[]{:S(2)}, u32[]{:S(2)}) collective-permute-start(bf16[192,640]{1,0:T(8,128)(2,1)S(1)} %collective-permute-done.23.b), channel_id=1, source_target_pairs={{0,2},{1,3},{2,0},{3,1},{4,6},{5,7},{6,4},{7,5},{8,10},{9,11},{10,... | collective-permute-start | bytes 737288 | tf_op jit(solution)/shard_map/ppermute | solution.py:48
  132.5 14.8 %collective-permute-start.29 = (bf16[480,768]{1,0:T(8,128)(2,1)S(1)}, bf16[480,768]{1,0:T(8,128)(2,1)S(1)}, u32[]{:S(2)}, u32[]{:S(2)}) collective-permute-start(bf16[480,768]{1,0:T(8,128)(2,1)S(1)} %collective-permute-done.27.a), channel_id=1, source_target_pairs={{0,2},{1,3},{2,0},{3,1},{4,6},{5,7},{6,4},{7,5},{8,10},{9,11},{10,... | collective-permute-start | bytes 2211848 | tf_op jit(solution)/shard_map/ppermute | solution.py:48
  133.1 14.3 %collective-permute-start.30 = (bf16[480,768]{1,0:T(8,128)(2,1)S(1)}, bf16[480,768]{1,0:T(8,128)(2,1)S(1)}, u32[]{:S(2)}, u32[]{:S(2)}) collective-permute-start(bf16[480,768]{1,0:T(8,128)(2,1)S(1)} %collective-permute-done.28.b), channel_id=1, source_target_pairs={{0,2},{1,3},{2,0},{3,1},{4,6},{5,7},{6,4},{7,5},{8,10},{9,11},{10,... | collective-permute-start | bytes 2211848 | tf_op jit(solution)/shard_map/ppermute | solution.py:48
  133.2 14.2 %collective-permute-start.26 = (bf16[384,512]{1,0:T(8,128)(2,1)S(1)}, bf16[384,512]{1,0:T(8,128)(2,1)S(1)}, u32[]{:S(2)}, u32[]{:S(2)}) collective-permute-start(bf16[384,512]{1,0:T(8,128)(2,1)S(1)} %get-tuple-element.90.kv), channel_id=1, source_target_pairs={{0,1},{1,2},{2,3},{3,4},{4,5},{5,6},{6,7},{7,8},{8,9},{9,10},{10,1... | collective-permute-start | bytes 1179656 | tf_op jit(solution)/shard_map/ppermute | solution.py:48
  (13 other events, 215.8 us)
where the time goes:
time: 163 us; the launch traced here: 162 us
  waiting for transfers between devices  60.8 us (37%)
  Pallas kernels  51.3 us (31%)
  starting transfers between devices  42.5 us (26%)
  local copies, waits for them, and re-layouts  5.61 us (3%)
    ppermute x31, waiting for transfers between devices, send(): return lax.ppermute(v, BOTH, p)  60.8 us
    pallas_call x6, Pallas kernels, call(): pl.pallas_call(body, out_shape=outs, in_specs=[spec for spec, _ in ins],...  46.8 us
    ppermute x31, starting transfers between devices, send(): return lax.ppermute(v, BOTH, p)  42.5 us
    pallas_call x1, Pallas kernels, cut(): pl.pallas_call(functools.partial(cut_kernel, parts), out_shape=shapes, in...  4.45 us
    unnamed x28, local copies, waits for them, and re-layouts  3.88 us
  transfers between devices with their start and end apart: 31, of which 15 were waited for; matrix products, arithmetic and copies ran while one was open for 1% of the time, Pallas kernels for 23%

commit v1 on v0

--- a/solution.py
+++ b/solution.py
@@ -75,13 +75,14 @@
     cur = jnp.where((pz == 4) | (pz == 5), got, cur)
     cur = jnp.concatenate([cur, send(cur, Z1)], axis=0)
     q1 = fetch(p[2], kv)
+    late = kv
     cur = jnp.concatenate([cur, send(cur, Y1)], axis=0)
     cur = jnp.concatenate([cur, send(cur, Y3)], axis=0)
     got = send(cur, CORE)
     whole = jnp.where(
         pc == 0, jnp.concatenate([cur, got], axis=1), jnp.concatenate([got, cur], axis=1)
     )
-    return whole, q, kv, prior, q0, r0, q1
+    return whole, q, kv, prior, q0, r0, q1, late
 
 
 VMEM = pl.BlockSpec(memory_space=pltpu.VMEM)
@@ -243,7 +244,6 @@
 
 
 QKV_STEP = 192
-MIX_STEP = 384
 END_STEP = 192
 WQ = jax.ShapeDtypeStruct((2 * D, G), BF)
 REST = [jax.ShapeDtypeStruct((n * D, D), BF) for n in (1, 2, 2)]
@@ -307,11 +307,13 @@
 
 
 def each_head(g, body, loop):
+    step = S // 2 if loop else S
+
     def one(h):
-        for row in range(0, S, MIX_STEP):
+        for row in range(0, S, step):
             body(
-                pl.ds(pl.multiple_of(h * S + row, MIX_STEP), MIX_STEP),
-                pl.ds(row, MIX_STEP),
+                pl.ds(pl.multiple_of(h * S + row, step), step),
+                pl.ds(row, step),
                 pl.ds(pl.multiple_of(h * HEAD, HEAD), HEAD),
             )
 
@@ -366,7 +368,7 @@
         def one(rows, to, lanes, columns=columns):
             acc, top = soften(q_ref[rows, :], (kv, prior), columns, shuts, ext)
             acc_ref[rows, :] = acc
-            top_ref[rows, :] = jnp.broadcast_to(top, (MIX_STEP, HEAD))
+            top_ref[rows, :] = jnp.broadcast_to(top, (top.shape[0], HEAD))
 
         each_head(g, one, True)
 
@@ -463,8 +465,8 @@
     for l in range(2):
         parts += [[(0, l, NQ)], [(1, l, NO), (2, l, NU), (3, l, NU)]]
     p = cut(info, (wqkv, *own), parts)
-    first, q, kv, prior, q0, r0, q1 = spread_first(x, p, joint)
-    r0 = swap(r0)
+    first, q, kv, prior, q0, r0, q1, late = spread_first(x, p, joint)
+    r0 = swap(r0, None)
     acc, top = call(
         begin_kernel,
         [jax.ShapeDtypeStruct((2 * RATIO * S, w), F32) for w in (2 * HEAD, HEAD)],
@@ -472,7 +474,7 @@
         8 * S * S * D,
         [ext_scratch(2)],
     )
-    r1 = fetch(p[3], first)
+    r1 = fetch(p[3], late)
     gains = [(VMEM, gain_a), (VMEM, gain_m)]
     x, kv0, wq, back, up, down = call(
         own_kernel,

time: 163 us -> 143 us (0.88)
  waiting for transfers between devices: 60.8 us -> 43.4 us
  Pallas kernels: 51.3 us -> 48.5 us
  local copies, waits for them, and re-layouts: 5.61 us -> 7.74 us
    ppermute x31, waiting for transfers between devices: 60.8 us -> 43.4 us  [send(): return lax.ppermute(v, BOTH, p)]
    pallas_call x6, Pallas kernels: 46.8 us -> 44.1 us  [call(): pl.pallas_call(body, out_shape=outs, in_specs=[spec for spec, _ in ins],...]
    unnamed x28 -> x30, local copies, waits for them, and re-layouts: 3.88 us -> 6.01 us
  transfers between devices with their start and end apart: 31 -> 31, of which waited for: 15 -> 14; matrix products, arithmetic and copies ran while one was open for 1% -> 1% of each run, Pallas kernels for 23% -> 25%
where the time goes in v1:
time: 143 us; the launch traced here: 142 us
  Pallas kernels  48.5 us (34%)
  waiting for transfers between devices  43.4 us (30%)
  starting transfers between devices  41.1 us (29%)
  local copies, waits for them, and re-layouts  7.74 us (5%)
    pallas_call x6, Pallas kernels, call(): pl.pallas_call(body, out_shape=outs, in_specs=[spec for spec, _ in ins],...  44.1 us
    ppermute x31, waiting for transfers between devices, send(): return lax.ppermute(v, BOTH, p)  43.4 us
    ppermute x31, starting transfers between devices, send(): return lax.ppermute(v, BOTH, p)  41.1 us
    unnamed x30, local copies, waits for them, and re-layouts  6.01 us
    pallas_call x1, Pallas kernels, cut(): pl.pallas_call(functools.partial(cut_kernel, parts), out_shape=shapes, in...  4.46 us
  transfers between devices with their start and end apart: 31, of which 14 were waited for; matrix products, arithmetic and copies ran while one was open for 1% of the time, Pallas kernels for 25%

profile of v1, /device:TPU:8, one launch (start us, length us, event | category | flops | bytes accessed | tf_op | source)
XLA Modules:
  0.0 142.1 jit_solution(1736372908570515820)
XLA Ops:
  0.0 1.7 %slice.33 = bf16[384,384]{1,0:T(8,128)(2,1)} slice(bf16[384,768]{1,0:T(8,128)(2,1)} %bitcast.5), slice={[0:384], [384:768]} | slice | bytes 589824 | tf_op jit(solution)/shard_map/slice | solution.py:56
  2.3 4.5 %cut.1 = (bf16[192,640]{1,0:T(8,128)(2,1)}, bf16[192,640]{1,0:T(8,128)(2,1)}, bf16[480,768]{1,0:T(8,128)(2,1)}, bf16[480,768]{1,0:T(8,128)(2,1)}, bf16[192,640]{...) custom-call(s32[3]{0:T(128)} %pad_add_fusion.info, ...), custom_call_target="tpu_custom_call" | custom-call | tf_op jit(solution)/shard_map/cut/pallas_call | solution.py:140
  6.9 1.7 %collective-permute-start.1 = (bf16[192,384]{1,0:T(8,128)(2,1)S(1)}, bf16[192,384]{1,0:T(8,128)(2,1)S(1)}, u32[]{:S(2)}, u32[]{:S(2)}) collective-permute-start(bf16[192,384]{1,0:T(8,128)(2,1)S(1)} %slice.27), channel_id=1, source_target_pairs={{0,12},{1,13},{2,14},{3,15},{4,8},{5,9},{6,10},{7,11},{8,4},{9,5},... | collective-permute-start | bytes 442376 | tf_op jit(solution)/shard_map/ppermute | solution.py:48
  8.6 4.7 %collective-permute-done.1 = bf16[192,384]{1,0:T(8,128)(2,1)S(1)} collective-permute-done((bf16[192,384]{1,0:T(8,128)(2,1)S(1)}, bf16[192,384]{1,0:T(8,128)(2,1)S(1)}, u32[]{:S(2)}, u32[]{:S(2)}) %collective-permute-start.1) | collective-permute-done | bytes 147488 | tf_op jit(solution)/shard_map/ppermute | solution.py:48
  13.3 3.5 %collective-permute-start.2 = (bf16[96,384]{1,0:T(8,128)(2,1)S(1)}, bf16[96,384]{1,0:T(8,128)(2,1)S(1)}, u32[]{:S(2)}, u32[]{:S(2)}) collective-permute-start(bf16[96,384]{1,0:T(8,128)(2,1)S(1)} %slice.35), channel_id=1, source_target_pairs={{0,4},{1,5},{2,6},{3,7},{4,0},{5,1},{6,2},{7,3},{8,12},{9,13},{10,... | collective-permute-start | bytes 221192 | tf_op jit(solution)/shard_map/ppermute | solution.py:48
  16.8 1.9 %collective-permute-start.4 = (bf16[192,640]{1,0:T(8,128)(2,1)}, bf16[192,640]{1,0:T(8,128)(2,1)S(1)}, u32[]{:S(2)}, u32[]{:S(2)}) collective-permute-start(bf16[192,640]{1,0:T(8,128)(2,1)} %get-tuple-element.63), channel_id=1, source_target_pairs={{0,129},{1,128},{2,131},{3,130},{4,133},{5,132},{6,135},{7,134},{8... | collective-permute-start | bytes 737288 | tf_op jit(solution)/shard_map/ppermute | solution.py:48
  19.1 5.1 %collective-permute-done.3.a.qa = bf16[192,640]{1,0:T(8,128)(2,1)S(1)} collective-permute-done((bf16[192,640]{1,0:T(8,128)(2,1)}, bf16[192,640]{1,0:T(8,128)(2,1)S(1)}, u32[]{:S(2)}, u32[]{:S(2)}) %collective-permute-start.3) | collective-permute-done | bytes 245792 | tf_op jit(solution)/shard_map/ppermute | solution.py:48
  25.4 1.5 %collective-permute-start.5 = (bf16[48,384]{1,0:T(8,128)(2,1)S(1)}, bf16[48,384]{1,0:T(8,128)(2,1)S(1)}, u32[]{:S(2)}, u32[]{:S(2)}) collective-permute-start(bf16[48,384]{1,0:T(8,128)(2,1)S(1)} %slice.31), channel_id=1, source_target_pairs={{0,16},{1,17},{2,18},{3,19},{4,20},{5,21},{6,22},{7,23},{8,24},{9,... | collective-permute-start | bytes 110600 | tf_op jit(solution)/shard_map/ppermute | solution.py:48
  27.0 2.4 %collective-permute-done.5 = bf16[48,384]{1,0:T(8,128)(2,1)S(1)} collective-permute-done((bf16[48,384]{1,0:T(8,128)(2,1)S(1)}, bf16[48,384]{1,0:T(8,128)(2,1)S(1)}, u32[]{:S(2)}, u32[]{:S(2)}) %collective-permute-start.5) | collective-permute-done | bytes 36896 | tf_op jit(solution)/shard_map/ppermute | solution.py:48
  30.5 2.9 %collective-permute-done.6 = bf16[48,384]{1,0:T(8,128)(2,1)S(1)} collective-permute-done((bf16[48,384]{1,0:T(8,128)(2,1)S(1)}, bf16[48,384]{1,0:T(8,128)(2,1)S(1)}, u32[]{:S(2)}, u32[]{:S(2)}) %collective-permute-start.6) | collective-permute-done | bytes 36896 | tf_op jit(solution)/shard_map/ppermute | solution.py:48
  33.5 1.8 %collective-permute-start.9 = (bf16[48,384]{1,0:T(8,128)(2,1)S(1)}, bf16[48,384]{1,0:T(8,128)(2,1)S(1)}, u32[]{:S(2)}, u32[]{:S(2)}) collective-permute-start(bf16[48,384]{1,0:T(8,128)(2,1)S(1)} %broadcast_select_fusion), channel_id=1, source_target_pairs={{0,129},{1,128},{2,131},{3,130},{4,133},{5,132},{6,135},{7,134},{8... | collective-permute-start | bytes 110600 | tf_op jit(solution)/shard_map/ppermute | solution.py:48
  35.3 3.6 %shard_map.82 = (bf16[2304,128]{1,0:T(8,128)(2,1)S(1)}, bf16[384,512]{1,0:T(8,128)(2,1)S(1)}) custom-call(s32[3]{0:T(128)S(1)} %copy-done.10, f32[2,6]{1,0:T(2,128)S(1)} %copy-done.11, bf16[384,768]{1,0:T(8,128)(2,1)S(1)} %bitcast.7, f32[2,768]{1,0:T(2,128)S(1)} %copy-done.9, bf16[2,768,640]{2,1,0:T(8,128)(2,1)S(1)} %copy-done, ...), custom_call_target="tpu_custom_call" | custom-call | flops 754974720 | bytes 8388608 | tf_op jit(solution)/shard_map/pallas_call | solution.py:284
  40.5 3.4 %collective-permute-start.10 = (bf16[48,384]{1,0:T(8,128)(2,1)S(1)}, bf16[48,384]{1,0:T(8,128)(2,1)S(1)}, u32[]{:S(2)}, u32[]{:S(2)}) collective-permute-start(bf16[48,384]{1,0:T(8,128)(2,1)S(1)} %broadcast_select_fusion.1), channel_id=1, source_target_pairs={{0,32},{1,33},{2,34},{3,35},{4,36},{5,37},{6,38},{7,39},{8,40},{9,... | collective-permute-start | bytes 110600 | tf_op jit(solution)/shard_map/ppermute | solution.py:48
  43.9 4.5 %collective-permute-start.11 = (bf16[48,384]{1,0:T(8,128)(2,1)S(1)}, bf16[48,384]{1,0:T(8,128)(2,1)S(1)}, u32[]{:S(2)}, u32[]{:S(2)}) collective-permute-start(bf16[48,384]{1,0:T(8,128)(2,1)S(1)} %broadcast_select_fusion.1), channel_id=1, source_target_pairs={{0,96},{1,97},{2,98},{3,99},{4,100},{5,101},{6,102},{7,103},{8,104... | collective-permute-start | bytes 110600 | tf_op jit(solution)/shard_map/ppermute | solution.py:48
  50.3 4.2 %collective-permute-start.12 = (bf16[48,384]{1,0:T(8,128)(2,1)S(1)}, bf16[48,384]{1,0:T(8,128)(2,1)S(1)}, u32[]{:S(2)}, u32[]{:S(2)}) collective-permute-start(bf16[48,384]{1,0:T(8,128)(2,1)S(1)} %select_select_fusion), channel_id=1, source_target_pairs={{0,96},{1,97},{2,98},{3,99},{4,100},{5,101},{6,102},{7,103},{8,104... | collective-permute-start | bytes 110600 | tf_op jit(solution)/shard_map/ppermute | solution.py:48
  54.5 2.0 %collective-permute-done.12 = bf16[48,384]{1,0:T(8,128)(2,1)S(1)} collective-permute-done((bf16[48,384]{1,0:T(8,128)(2,1)S(1)}, bf16[48,384]{1,0:T(8,128)(2,1)S(1)}, u32[]{:S(2)}, u32[]{:S(2)}) %collective-permute-start.12) | collective-permute-done | bytes 36896 | tf_op jit(solution)/shard_map/ppermute | solution.py:48
  56.5 1.9 %collective-permute-start.13 = (bf16[48,384]{1,0:T(8,128)(2,1)S(1)}, bf16[48,384]{1,0:T(8,128)(2,1)S(1)}, u32[]{:S(2)}, u32[]{:S(2)}) collective-permute-start(bf16[48,384]{1,0:T(8,128)(2,1)S(1)} %broadcast_select_fusion.2), channel_id=1, source_target_pairs={{0,16},{1,17},{2,18},{3,19},{4,20},{5,21},{6,22},{7,23},{8,24},{9,... | collective-permute-start | bytes 110600 | tf_op jit(solution)/shard_map/ppermute | solution.py:48
  58.4 2.1 %collective-permute-done.13 = bf16[48,384]{1,0:T(8,128)(2,1)S(1)} collective-permute-done((bf16[48,384]{1,0:T(8,128)(2,1)S(1)}, bf16[48,384]{1,0:T(8,128)(2,1)S(1)}, u32[]{:S(2)}, u32[]{:S(2)}) %collective-permute-start.13) | collective-permute-done | bytes 36896 | tf_op jit(solution)/shard_map/ppermute | solution.py:48
  61.0 3.4 %collective-permute-done.18.a = bf16[480,768]{1,0:T(8,128)(2,1)} collective-permute-done((bf16[480,768]{1,0:T(8,128)(2,1)}, bf16[480,768]{1,0:T(8,128)(2,1)}, u32[]{:S(2)}, u32[]{:S(2)}) %collective-permute-start.18) | collective-permute-done | bytes 737312 | tf_op jit(solution)/shard_map/ppermute | solution.py:48
  64.4 2.2 %collective-permute-done.19.b = bf16[480,768]{1,0:T(8,128)(2,1)} collective-permute-done((bf16[480,768]{1,0:T(8,128)(2,1)}, bf16[480,768]{1,0:T(8,128)(2,1)}, u32[]{:S(2)}, u32[]{:S(2)}) %collective-permute-start.19) | collective-permute-done | bytes 737312 | tf_op jit(solution)/shard_map/ppermute | solution.py:48
  66.7 2.4 %collective-permute-start.15 = (bf16[192,384]{1,0:T(8,128)(2,1)S(1)}, bf16[192,384]{1,0:T(8,128)(2,1)S(1)}, u32[]{:S(2)}, u32[]{:S(2)}) collective-permute-start(bf16[192,384]{1,0:T(8,128)(2,1)S(1)} %pad_maximum_fusion.1), channel_id=1, source_target_pairs={{0,12},{1,13},{2,14},{3,15},{4,8},{5,9},{6,10},{7,11},{8,4},{9,5},... | collective-permute-start | bytes 442376 | tf_op jit(solution)/shard_map/ppermute | solution.py:48
  69.0 1.9 %collective-permute-start.17 = (bf16[384,512]{1,0:T(8,128)(2,1)}, bf16[384,512]{1,0:T(8,128)(2,1)S(1)}, u32[]{:S(2)}, u32[]{:S(2)}) collective-permute-start(bf16[384,512]{1,0:T(8,128)(2,1)} %copy-done.13), channel_id=1, source_target_pairs={{0,1},{1,2},{2,3},{3,4},{4,5},{5,6},{6,7},{7,8},{8,9},{9,10},{10,1... | collective-permute-start | bytes 1179656 | tf_op jit(solution)/shard_map/ppermute | solution.py:48
  70.9 1.9 %collective-permute-start.22 = (bf16[192,640]{1,0:T(8,128)(2,1)}, bf16[192,640]{1,0:T(8,128)(2,1)S(1)}, u32[]{:S(2)}, u32[]{:S(2)}) collective-permute-start(bf16[192,640]{1,0:T(8,128)(2,1)} %get-tuple-element.85), channel_id=1, source_target_pairs={{0,1},{1,0},{2,3},{3,2},{4,5},{5,4},{6,7},{7,6},{8,9},{9,8},{10,11... | collective-permute-start | bytes 737288 | tf_op jit(solution)/shard_map/ppermute | solution.py:48
  74.7 12.6 %collective-permute-done.22.a = bf16[192,640]{1,0:T(8,128)(2,1)S(1)} collective-permute-done((bf16[192,640]{1,0:T(8,128)(2,1)}, bf16[192,640]{1,0:T(8,128)(2,1)S(1)}, u32[]{:S(2)}, u32[]{:S(2)}) %collective-permute-start.22) | collective-permute-done | bytes 245792 | tf_op jit(solution)/shard_map/ppermute | solution.py:48
  91.1 5.0 %shard_map.83 = (f32[2304,256]{1,0:T(8,128)S(1)}, f32[2304,128]{1,0:T(8,128)S(1)}) custom-call(s32[3]{0:T(128)S(1)} %copy-done.10, bf16[2304,128]{1,0:T(8,128)(2,1)S(1)} %copy-done.7, bf16[384,512]{1,0:T(8,128)(2,1)S(1)} %copy-done.14, bf16[384,512]{1,0:T(8,128)(2,1)S(1)} %collective-permute-done.17.prior), custom_call_target="tpu_custom_call" | custom-call | flops 905969664 | bytes 8388608 | tf_op jit(solution)/shard_map/pallas_call | solution.py:284
  97.3 1.3 copy-done.4
  99.6 10.7 %shard_map.84 = (bf16[384,768]{1,0:T(8,128)(2,1)S(1)}, bf16[384,512]{1,0:T(8,128)(2,1)S(1)}, bf16[1536,640]{1,0:T(8,128)(2,1)S(1)}, bf16[768,768]{1,0:T(8,128)(2...) custom-call(s32[3]{0:T(128)S(1)} %copy-done.10, f32[2,6]{1,0:T(2,128)S(1)} %copy-done.11, ...), custom_call_target="tpu_custom_call" | custom-call | flops 3623878656 | bytes 8388608 | tf_op jit(solution)/shard_map/pallas_call | solution.py:284
  110.3 3.9 %shard_map.85 = (bf16[2304,128]{1,0:T(8,128)(2,1)S(1)}, bf16[384,512]{1,0:T(8,128)(2,1)S(1)}, bf16[1536,640]{1,0:T(8,128)(2,1)S(1)}) custom-call(s32[3]{0:T(128)S(1)} %copy-done.10, f32[2,6]{1,0:T(2,128)S(1)} %copy-done.11, bf16[384,768]{1,0:T(8,128)(2,1)S(1)} %get-tuple-element.82.x_ref, f32[2,768]{1,0:T(2,128)S(1)} %copy-done.9, ...), custom_call_target="tpu_custom_call" | custom-call | flops 754974720 | bytes 8388608 | tf_op jit(solution)/shard_map/pallas_call | solution.py:284
  114.8 3.3 %collective-permute-start.26 = (bf16[384,512]{1,0:T(8,128)(2,1)S(1)}, bf16[384,512]{1,0:T(8,128)(2,1)S(1)}, u32[]{:S(2)}, u32[]{:S(2)}) collective-permute-start(bf16[384,512]{1,0:T(8,128)(2,1)S(1)} %get-tuple-element.90.kv), channel_id=1, source_target_pairs={{0,1},{1,2},{2,3},{3,4},{4,5},{5,6},{6,7},{7,8},{8,9},{9,10},{10,1... | collective-permute-start | bytes 1179656 | tf_op jit(solution)/shard_map/ppermute | solution.py:48
  118.1 7.9 %shard_map.86.kv0 = bf16[384,512]{1,0:T(8,128)(2,1)S(1)} custom-call(s32[3]{0:T(128)S(1)} %copy-done.10, f32[2,6]{1,0:T(2,128)S(1)} %copy-done.11, bf16[384,768]{1,0:T(8,128)(2,1)S(1)} %maximum_select_fusion.first, bf16[384,512]{1,0:T(8,128)(2,1)S(1)} %get-tuple-element.91.kv0, f32[2,768]{1,0:T(2,128)S(1)} %copy-done.9, f32[2,768]{1,0:T(2,128)S(1)} %copy-done.12, ...), custom_call_target="tpu_custom_call" | custom-call | flops 3623878656 | bytes 8388608 | tf_op jit(solution)/shard_map/pallas_call | solution.py:284
  126.1 2.9 %collective-permute-done.26.prior = bf16[384,512]{1,0:T(8,128)(2,1)S(1)} collective-permute-done((bf16[384,512]{1,0:T(8,128)(2,1)S(1)}, bf16[384,512]{1,0:T(8,128)(2,1)S(1)}, u32[]{:S(2)}, u32[]{:S(2)}) %collective-permute-start.26) | collective-permute-done | bytes 393248 | tf_op jit(solution)/shard_map/ppermute | solution.py:48
  129.0 12.9 %shard_map.87 = bf16[384,768]{1,0:T(8,128)(2,1)} custom-call(s32[3]{0:T(128)S(1)} %copy-done.10, bf16[384,768]{1,0:T(8,128)(2,1)S(1)} %get-tuple-element.82.x_ref, bf16[2304,128]{1,0:T(8,128)(2,1)S(1)} %get-tuple-element.89.q_ref, bf16[384,512]{1,0:T(8,128)(2,1)S(1)} %get-tuple-element.90.kv, bf16[384,512]{1,0:T(8,128)(2,1)S(1)} %collective-permute-done.26.prior, ...), custom_call_target="tpu_custom_call" | custom-call | flops 3623878656 | bytes 8388608 | tf_op jit(solution)/shard_map/pallas_call | solution.py:284
  (84 shorter events, 16.0 us)
Async XLA Ops:
  1.7 5.1 %collective-permute-start = (bf16[384,384]{1,0:T(8,128)(2,1)}, bf16[384,384]{1,0:T(8,128)(2,1)S(1)}, u32[]{:S(2)}, u32[]{:S(2)}) collective-permute-start(bf16[384,384]{1,0:T(8,128)(2,1)} %slice.33), channel_id=1, source_target_pairs={{0,2},{1,3},{2,0},{3,1},{4,6},{5,7},{6,4},{7,5},{8,10},{9,11},{10,... | collective-permute-start | bytes 884744 | tf_op jit(solution)/shard_map/ppermute | solution.py:48
  6.8 28.5 %copy-start = (bf16[2,768,640]{2,1,0:T(8,128)(2,1)S(1)}, bf16[2,768,640]{2,1,0:T(8,128)(2,1)}, u32[]{:S(2)}) copy-start(bf16[2,768,640]{2,1,0:T(8,128)(2,1)} %wq.3) | copy-start | bytes 5898244
  6.9 6.3 %collective-permute-start.1 = (bf16[192,384]{1,0:T(8,128)(2,1)S(1)}, bf16[192,384]{1,0:T(8,128)(2,1)S(1)}, u32[]{:S(2)}, u32[]{:S(2)}) collective-permute-start(bf16[192,384]{1,0:T(8,128)(2,1)S(1)} %slice.27), channel_id=1, source_target_pairs={{0,12},{1,13},{2,14},{3,15},{4,8},{5,9},{6,10},{7,11},{8,4},{9,5},... | collective-permute-start | bytes 442376 | tf_op jit(solution)/shard_map/ppermute | solution.py:48
  13.3 5.8 %collective-permute-start.2 = (bf16[96,384]{1,0:T(8,128)(2,1)S(1)}, bf16[96,384]{1,0:T(8,128)(2,1)S(1)}, u32[]{:S(2)}, u32[]{:S(2)}) collective-permute-start(bf16[96,384]{1,0:T(8,128)(2,1)S(1)} %slice.35), channel_id=1, source_target_pairs={{0,4},{1,5},{2,6},{3,7},{4,0},{5,1},{6,2},{7,3},{8,12},{9,13},{10,... | collective-permute-start | bytes 221192 | tf_op jit(solution)/shard_map/ppermute | solution.py:48
  16.7 7.4 %collective-permute-start.3 = (bf16[192,640]{1,0:T(8,128)(2,1)}, bf16[192,640]{1,0:T(8,128)(2,1)S(1)}, u32[]{:S(2)}, u32[]{:S(2)}) collective-permute-start(bf16[192,640]{1,0:T(8,128)(2,1)} %get-tuple-element.62), channel_id=1, source_target_pairs={{0,1},{1,0},{2,3},{3,2},{4,5},{5,4},{6,7},{7,6},{8,9},{9,8},{10,11... | collective-permute-start | bytes 737288 | tf_op jit(solution)/shard_map/ppermute | solution.py:48
  16.8 8.7 %collective-permute-start.4 = (bf16[192,640]{1,0:T(8,128)(2,1)}, bf16[192,640]{1,0:T(8,128)(2,1)S(1)}, u32[]{:S(2)}, u32[]{:S(2)}) collective-permute-start(bf16[192,640]{1,0:T(8,128)(2,1)} %get-tuple-element.63), channel_id=1, source_target_pairs={{0,129},{1,128},{2,131},{3,130},{4,133},{5,132},{6,135},{7,134},{8... | collective-permute-start | bytes 737288 | tf_op jit(solution)/shard_map/ppermute | solution.py:48
  25.4 4.0 %collective-permute-start.5 = (bf16[48,384]{1,0:T(8,128)(2,1)S(1)}, bf16[48,384]{1,0:T(8,128)(2,1)S(1)}, u32[]{:S(2)}, u32[]{:S(2)}) collective-permute-start(bf16[48,384]{1,0:T(8,128)(2,1)S(1)} %slice.31), channel_id=1, source_target_pairs={{0,16},{1,17},{2,18},{3,19},{4,20},{5,21},{6,22},{7,23},{8,24},{9,... | collective-permute-start | bytes 110600 | tf_op jit(solution)/shard_map/ppermute | solution.py:48
  29.4 4.0 %collective-permute-start.6 = (bf16[48,384]{1,0:T(8,128)(2,1)S(1)}, bf16[48,384]{1,0:T(8,128)(2,1)S(1)}, u32[]{:S(2)}, u32[]{:S(2)}) collective-permute-start(bf16[48,384]{1,0:T(8,128)(2,1)S(1)} %slice_select_fusion.3), channel_id=1, source_target_pairs={{0,1},{1,0},{2,3},{3,2},{4,5},{5,4},{6,7},{7,6},{8,9},{9,8},{10,11... | collective-permute-start | bytes 110600 | tf_op jit(solution)/shard_map/ppermute | solution.py:48
  30.0 3.4 %collective-permute-start.7 = (bf16[192,640]{1,0:T(8,128)(2,1)S(1)}, bf16[192,640]{1,0:T(8,128)(2,1)S(1)}, u32[]{:S(2)}, u32[]{:S(2)}) collective-permute-start(bf16[192,640]{1,0:T(8,128)(2,1)S(1)} %collective-permute-done.3.a.qa), channel_id=1, source_target_pairs={{0,2},{1,3},{2,0},{3,1},{4,6},{5,7},{6,4},{7,5},{8,10},{9,11},{10,... | collective-permute-start | bytes 737288 | tf_op jit(solution)/shard_map/ppermute | solution.py:48
  30.0 3.4 %collective-permute-start.8 = (bf16[192,640]{1,0:T(8,128)(2,1)S(1)}, bf16[192,640]{1,0:T(8,128)(2,1)}, u32[]{:S(2)}, u32[]{:S(2)}) collective-permute-start(bf16[192,640]{1,0:T(8,128)(2,1)S(1)} %collective-permute-done.4.b.qb), channel_id=1, source_target_pairs={{0,2},{1,3},{2,0},{3,1},{4,6},{5,7},{6,4},{7,5},{8,10},{9,11},{10,... | collective-permute-start | bytes 737288 | tf_op jit(solution)/shard_map/ppermute | solution.py:48
  33.5 7.0 %collective-permute-start.9 = (bf16[48,384]{1,0:T(8,128)(2,1)S(1)}, bf16[48,384]{1,0:T(8,128)(2,1)S(1)}, u32[]{:S(2)}, u32[]{:S(2)}) collective-permute-start(bf16[48,384]{1,0:T(8,128)(2,1)S(1)} %broadcast_select_fusion), channel_id=1, source_target_pairs={{0,129},{1,128},{2,131},{3,130},{4,133},{5,132},{6,135},{7,134},{8... | collective-permute-start | bytes 110600 | tf_op jit(solution)/shard_map/ppermute | solution.py:48
  40.5 9.0 %collective-permute-start.10 = (bf16[48,384]{1,0:T(8,128)(2,1)S(1)}, bf16[48,384]{1,0:T(8,128)(2,1)S(1)}, u32[]{:S(2)}, u32[]{:S(2)}) collective-permute-start(bf16[48,384]{1,0:T(8,128)(2,1)S(1)} %broadcast_select_fusion.1), channel_id=1, source_target_pairs={{0,32},{1,33},{2,34},{3,35},{4,36},{5,37},{6,38},{7,39},{8,40},{9,... | collective-permute-start | bytes 110600 | tf_op jit(solution)/shard_map/ppermute | solution.py:48
  43.9 6.4 %collective-permute-start.11 = (bf16[48,384]{1,0:T(8,128)(2,1)S(1)}, bf16[48,384]{1,0:T(8,128)(2,1)S(1)}, u32[]{:S(2)}, u32[]{:S(2)}) collective-permute-start(bf16[48,384]{1,0:T(8,128)(2,1)S(1)} %broadcast_select_fusion.1), channel_id=1, source_target_pairs={{0,96},{1,97},{2,98},{3,99},{4,100},{5,101},{6,102},{7,103},{8,104... | collective-permute-start | bytes 110600 | tf_op jit(solution)/shard_map/ppermute | solution.py:48
  48.3 16.0 %collective-permute-start.18 = (bf16[480,768]{1,0:T(8,128)(2,1)}, bf16[480,768]{1,0:T(8,128)(2,1)}, u32[]{:S(2)}, u32[]{:S(2)}) collective-permute-start(bf16[480,768]{1,0:T(8,128)(2,1)} %get-tuple-element.80), channel_id=1, source_target_pairs={{0,1},{1,0},{2,3},{3,2},{4,5},{5,4},{6,7},{7,6},{8,9},{9,8},{10,11... | collective-permute-start | bytes 2211848 | tf_op jit(solution)/shard_map/ppermute | solution.py:48
  48.3 18.3 %collective-permute-start.19 = (bf16[480,768]{1,0:T(8,128)(2,1)}, bf16[480,768]{1,0:T(8,128)(2,1)}, u32[]{:S(2)}, u32[]{:S(2)}) collective-permute-start(bf16[480,768]{1,0:T(8,128)(2,1)} %get-tuple-element.81), channel_id=1, source_target_pairs={{0,129},{1,128},{2,131},{3,130},{4,133},{5,132},{6,135},{7,134},{8... | collective-permute-start | bytes 2211848 | tf_op jit(solution)/shard_map/ppermute | solution.py:48
  50.3 6.2 %collective-permute-start.12 = (bf16[48,384]{1,0:T(8,128)(2,1)S(1)}, bf16[48,384]{1,0:T(8,128)(2,1)S(1)}, u32[]{:S(2)}, u32[]{:S(2)}) collective-permute-start(bf16[48,384]{1,0:T(8,128)(2,1)S(1)} %select_select_fusion), channel_id=1, source_target_pairs={{0,96},{1,97},{2,98},{3,99},{4,100},{5,101},{6,102},{7,103},{8,104... | collective-permute-start | bytes 110600 | tf_op jit(solution)/shard_map/ppermute | solution.py:48
  56.5 4.0 %collective-permute-start.13 = (bf16[48,384]{1,0:T(8,128)(2,1)S(1)}, bf16[48,384]{1,0:T(8,128)(2,1)S(1)}, u32[]{:S(2)}, u32[]{:S(2)}) collective-permute-start(bf16[48,384]{1,0:T(8,128)(2,1)S(1)} %broadcast_select_fusion.2), channel_id=1, source_target_pairs={{0,16},{1,17},{2,18},{3,19},{4,20},{5,21},{6,22},{7,23},{8,24},{9,... | collective-permute-start | bytes 110600 | tf_op jit(solution)/shard_map/ppermute | solution.py:48
  60.5 6.1 %collective-permute-start.14 = (bf16[96,384]{1,0:T(8,128)(2,1)S(1)}, bf16[96,384]{1,0:T(8,128)(2,1)S(1)}, u32[]{:S(2)}, u32[]{:S(2)}) collective-permute-start(bf16[96,384]{1,0:T(8,128)(2,1)S(1)} %pad_maximum_fusion.2), channel_id=1, source_target_pairs={{0,4},{1,5},{2,6},{3,7},{4,0},{5,1},{6,2},{7,3},{8,12},{9,13},{10,... | collective-permute-start | bytes 221192 | tf_op jit(solution)/shard_map/ppermute | solution.py:48
  64.4 32.1 %collective-permute-start.20 = (bf16[480,768]{1,0:T(8,128)(2,1)}, bf16[480,768]{1,0:T(8,128)(2,1)S(1)}, u32[]{:S(2)}, u32[]{:S(2)}) collective-permute-start(bf16[480,768]{1,0:T(8,128)(2,1)} %collective-permute-done.18.a), channel_id=1, source_target_pairs={{0,2},{1,3},{2,0},{3,1},{4,6},{5,7},{6,4},{7,5},{8,10},{9,11},{10,... | collective-permute-start | bytes 2211848 | tf_op jit(solution)/shard_map/ppermute | solution.py:48
  66.6 30.6 %collective-permute-start.21 = (bf16[480,768]{1,0:T(8,128)(2,1)}, bf16[480,768]{1,0:T(8,128)(2,1)S(1)}, u32[]{:S(2)}, u32[]{:S(2)}) collective-permute-start(bf16[480,768]{1,0:T(8,128)(2,1)} %collective-permute-done.19.b), channel_id=1, source_target_pairs={{0,2},{1,3},{2,0},{3,1},{4,6},{5,7},{6,4},{7,5},{8,10},{9,11},{10,... | collective-permute-start | bytes 2211848 | tf_op jit(solution)/shard_map/ppermute | solution.py:48
  66.7 6.9 %collective-permute-start.15 = (bf16[192,384]{1,0:T(8,128)(2,1)S(1)}, bf16[192,384]{1,0:T(8,128)(2,1)S(1)}, u32[]{:S(2)}, u32[]{:S(2)}) collective-permute-start(bf16[192,384]{1,0:T(8,128)(2,1)S(1)} %pad_maximum_fusion.1), channel_id=1, source_target_pairs={{0,12},{1,13},{2,14},{3,15},{4,8},{5,9},{6,10},{7,11},{8,4},{9,5},... | collective-permute-start | bytes 442376 | tf_op jit(solution)/shard_map/ppermute | solution.py:48
  69.0 18.9 %collective-permute-start.17 = (bf16[384,512]{1,0:T(8,128)(2,1)}, bf16[384,512]{1,0:T(8,128)(2,1)S(1)}, u32[]{:S(2)}, u32[]{:S(2)}) collective-permute-start(bf16[384,512]{1,0:T(8,128)(2,1)} %copy-done.13), channel_id=1, source_target_pairs={{0,1},{1,2},{2,3},{3,4},{4,5},{5,6},{6,7},{7,8},{8,9},{9,10},{10,1... | collective-permute-start | bytes 1179656 | tf_op jit(solution)/shard_map/ppermute | solution.py:48
  70.9 16.3 %collective-permute-start.22 = (bf16[192,640]{1,0:T(8,128)(2,1)}, bf16[192,640]{1,0:T(8,128)(2,1)S(1)}, u32[]{:S(2)}, u32[]{:S(2)}) collective-permute-start(bf16[192,640]{1,0:T(8,128)(2,1)} %get-tuple-element.85), channel_id=1, source_target_pairs={{0,1},{1,0},{2,3},{3,2},{4,5},{5,4},{6,7},{7,6},{8,9},{9,8},{10,11... | collective-permute-start | bytes 737288 | tf_op jit(solution)/shard_map/ppermute | solution.py:48
  73.5 13.7 %collective-permute-start.23 = (bf16[192,640]{1,0:T(8,128)(2,1)}, bf16[192,640]{1,0:T(8,128)(2,1)S(1)}, u32[]{:S(2)}, u32[]{:S(2)}) collective-permute-start(bf16[192,640]{1,0:T(8,128)(2,1)} %get-tuple-element.86), channel_id=1, source_target_pairs={{0,129},{1,128},{2,131},{3,130},{4,133},{5,132},{6,135},{7,134},{8... | collective-permute-start | bytes 737288 | tf_op jit(solution)/shard_map/ppermute | solution.py:48
  87.3 8.9 %collective-permute-start.16 = (bf16[384,384]{1,0:T(8,128)(2,1)S(1)}, bf16[384,384]{1,0:T(8,128)(2,1)S(1)}, u32[]{:S(2)}, u32[]{:S(2)}) collective-permute-start(bf16[384,384]{1,0:T(8,128)(2,1)S(1)} %pad_maximum_fusion), channel_id=1, source_target_pairs={{0,2},{1,3},{2,0},{3,1},{4,6},{5,7},{6,4},{7,5},{8,10},{9,11},{10,... | collective-permute-start | bytes 884744 | tf_op jit(solution)/shard_map/ppermute | solution.py:48
  87.3 26.9 %collective-permute-start.27 = (bf16[480,768]{1,0:T(8,128)(2,1)}, bf16[480,768]{1,0:T(8,128)(2,1)S(1)}, u32[]{:S(2)}, u32[]{:S(2)}) collective-permute-start(bf16[480,768]{1,0:T(8,128)(2,1)} %get-tuple-element.97), channel_id=1, source_target_pairs={{0,1},{1,0},{2,3},{3,2},{4,5},{5,4},{6,7},{7,6},{8,9},{9,8},{10,11... | collective-permute-start | bytes 2211848 | tf_op jit(solution)/shard_map/ppermute | solution.py:48
  87.9 26.3 %collective-permute-start.28 = (bf16[480,768]{1,0:T(8,128)(2,1)}, bf16[480,768]{1,0:T(8,128)(2,1)S(1)}, u32[]{:S(2)}, u32[]{:S(2)}) collective-permute-start(bf16[480,768]{1,0:T(8,128)(2,1)} %get-tuple-element.98), channel_id=1, source_target_pairs={{0,129},{1,128},{2,131},{3,130},{4,133},{5,132},{6,135},{7,134},{8... | collective-permute-start | bytes 2211848 | tf_op jit(solution)/shard_map/ppermute | solution.py:48
  96.2 14.1 %collective-permute-start.24 = (bf16[192,640]{1,0:T(8,128)(2,1)S(1)}, bf16[192,640]{1,0:T(8,128)(2,1)S(1)}, u32[]{:S(2)}, u32[]{:S(2)}) collective-permute-start(bf16[192,640]{1,0:T(8,128)(2,1)S(1)} %collective-permute-done.22.a), channel_id=1, source_target_pairs={{0,2},{1,3},{2,0},{3,1},{4,6},{5,7},{6,4},{7,5},{8,10},{9,11},{10,... | collective-permute-start | bytes 737288 | tf_op jit(solution)/shard_map/ppermute | solution.py:48
  96.5 13.9 %collective-permute-start.25 = (bf16[192,640]{1,0:T(8,128)(2,1)S(1)}, bf16[192,640]{1,0:T(8,128)(2,1)S(1)}, u32[]{:S(2)}, u32[]{:S(2)}) collective-permute-start(bf16[192,640]{1,0:T(8,128)(2,1)S(1)} %collective-permute-done.23.b), channel_id=1, source_target_pairs={{0,2},{1,3},{2,0},{3,1},{4,6},{5,7},{6,4},{7,5},{8,10},{9,11},{10,... | collective-permute-start | bytes 737288 | tf_op jit(solution)/shard_map/ppermute | solution.py:48
  114.2 14.7 %collective-permute-start.29 = (bf16[480,768]{1,0:T(8,128)(2,1)S(1)}, bf16[480,768]{1,0:T(8,128)(2,1)S(1)}, u32[]{:S(2)}, u32[]{:S(2)}) collective-permute-start(bf16[480,768]{1,0:T(8,128)(2,1)S(1)} %collective-permute-done.27.a), channel_id=1, source_target_pairs={{0,2},{1,3},{2,0},{3,1},{4,6},{5,7},{6,4},{7,5},{8,10},{9,11},{10,... | collective-permute-start | bytes 2211848 | tf_op jit(solution)/shard_map/ppermute | solution.py:48
  114.4 14.6 %collective-permute-start.30 = (bf16[480,768]{1,0:T(8,128)(2,1)S(1)}, bf16[480,768]{1,0:T(8,128)(2,1)S(1)}, u32[]{:S(2)}, u32[]{:S(2)}) collective-permute-start(bf16[480,768]{1,0:T(8,128)(2,1)S(1)} %collective-permute-done.28.b), channel_id=1, source_target_pairs={{0,2},{1,3},{2,0},{3,1},{4,6},{5,7},{6,4},{7,5},{8,10},{9,11},{10,... | collective-permute-start | bytes 2211848 | tf_op jit(solution)/shard_map/ppermute | solution.py:48
  114.8 14.1 %collective-permute-start.26 = (bf16[384,512]{1,0:T(8,128)(2,1)S(1)}, bf16[384,512]{1,0:T(8,128)(2,1)S(1)}, u32[]{:S(2)}, u32[]{:S(2)}) collective-permute-start(bf16[384,512]{1,0:T(8,128)(2,1)S(1)} %get-tuple-element.90.kv), channel_id=1, source_target_pairs={{0,1},{1,2},{2,3},{3,4},{4,5},{5,6},{6,7},{7,8},{8,9},{9,10},{10,1... | collective-permute-start | bytes 1179656 | tf_op jit(solution)/shard_map/ppermute | solution.py:48
  (14 other events, 136.6 us)
